TPU v7x, 128 devices: a whole 4x4x4 slice. The times are simulated.
128 devices in a mesh: front: 4 (over y), row: 8 (over z, x_lo), col: 4 (over x_hi, core).
Axes of the slice: x: 4 (x_hi: 2, x_lo: 2; x = x_hi * 2 + x_lo), y: 4, z: 4, core: 2. Of those that a mesh axis runs over, the one named last changes fastest.
Arguments:
- front_entries: bfloat16 [36864, 9216], P(('front', 'row'), 'col'), parts along dimension 0, as said below
- children: bfloat16 [8, 8192, 8192], P('front', 'row', 'col'), parts along dimension 0, as said below
- child_maps: int32 [8, 64], P('front'), parts along dimension 0, may hold values from 0 to 71, as said below
Outputs:
- factor: float32 [36864, 9216], P(('front', 'row'), 'col'), parts along dimension 0
There are 4 independent parts, one for each index of `front`. A program takes and returns all parts, laid end to end along the dimension named above; each array names one. Nothing has to cross between parts.
Inputs may be any that keep to these rules, and one draw needn't show every extreme that they name: `front_entries`: symmetric in natural order; the leading 256 x 256 block of the matrix assembled by the steps is positive definite. `children`: each child's matrix is symmetric in natural order. `child_maps`: the entries of one child are distinct. For each child, among its blocks k with k mod 8 = a, exactly 1 has a value v with v mod 8 = d, for every a and d; and among its blocks k with k mod 4 = a, exactly 4 have a value v with v mod 4 = d, for every a and d.
All inputs are finite; a program needn't handle non-finite values.
Results may differ from a plain program's by a relative error of at most 0.0003.
Values may be sent and summed in bfloat16 or wider, within the bound.
A program may use at most 128 MiB of HBM per device.

v0:
```python
import jax
import jax.numpy as jnp
from jax import lax
from jax.sharding import PartitionSpec as P

BLK = 128
SEP = 256


def broadcast(value, axis, source):
    kept = jnp.where(lax.axis_index(axis) == source, value, 0).astype(value.dtype)
    return lax.psum(kept, axis)


def arrivals(child_maps, axis_size, own_index, blocks):
    local_ids = jnp.arange(blocks, dtype=jnp.int32)
    source = jnp.arange(axis_size, dtype=jnp.int32)
    parents = child_maps[:, local_ids[None, :] * axis_size + source[:, None]]
    ranking = jnp.argsort(
        jnp.where(parents % axis_size == own_index, 0, 1) * blocks + local_ids, axis=2
    )
    chosen = jnp.take_along_axis(parents, ranking[:, :, : blocks // axis_size], axis=2)
    return (chosen // axis_size).reshape(parents.shape[0], -1)


def sending_order(child_maps, axis_size, own_index, blocks):
    local_ids = jnp.arange(blocks, dtype=jnp.int32)
    parents = child_maps[:, local_ids * axis_size + own_index]
    return jnp.argsort(parents % axis_size * blocks + local_ids[None, :], axis=1)


def shards(front_entries, children, child_maps):
    rows_axis = lax.axis_size("row")
    cols_axis = lax.axis_size("col")
    own_row = lax.axis_index("row")
    own_col = lax.axis_index("col")
    front_rows = front_entries.shape[0] // BLK
    front_cols = front_entries.shape[1] // BLK
    child_rows = children.shape[1] // BLK
    child_cols = children.shape[2] // BLK
    row_sends = child_rows // rows_axis
    col_sends = child_cols // cols_axis
    row_order = sending_order(child_maps, rows_axis, own_row, child_rows)
    col_order = sending_order(child_maps, cols_axis, own_col, child_cols)
    tile_grid = children.reshape(2, child_rows, BLK, child_cols, BLK)
    tile_grid = jnp.take_along_axis(tile_grid, row_order[:, :, None, None, None], axis=1)
    tile_grid = jnp.take_along_axis(tile_grid, col_order[:, None, None, :, None], axis=3)
    tile_grid = tile_grid.reshape(2, rows_axis, row_sends, BLK, cols_axis, col_sends, BLK)
    outgoing = tile_grid.transpose(0, 1, 4, 2, 3, 5, 6).reshape(
        2, rows_axis * cols_axis, row_sends, BLK, col_sends, BLK
    )
    incoming = lax.all_to_all(outgoing, ("row", "col"), split_axis=1, concat_axis=1, tiled=True)
    incoming = incoming.reshape(2, rows_axis, cols_axis, row_sends, BLK, col_sends, BLK)
    arrived = incoming.transpose(0, 1, 3, 4, 2, 5, 6)
    arrived = arrived.reshape(2, child_rows, BLK, child_cols, BLK)
    row_dest = arrivals(child_maps, rows_axis, own_row, child_rows)
    col_dest = arrivals(child_maps, cols_axis, own_col, child_cols)
    assembled = front_entries.astype(jnp.float32).reshape(front_rows, BLK, front_cols, BLK)
    for child_index in range(2):
        addend = arrived[child_index].transpose(0, 2, 1, 3).astype(jnp.float32)
        assembled = assembled.at[
            row_dest[child_index][:, None], :, col_dest[child_index][None, :], :
        ].add(addend)
    assembled = assembled.reshape(front_rows * BLK, front_cols * BLK)
    row_blocks = jnp.arange(front_rows, dtype=jnp.int32) * rows_axis + own_row
    col_blocks = jnp.arange(front_cols, dtype=jnp.int32) * cols_axis + own_col
    spread = rows_axis // cols_axis

    def eliminate(pivot_index, current_front):
        col_slot = pivot_index // cols_axis
        column = lax.dynamic_slice_in_dim(current_front, col_slot * BLK, BLK, 1)
        column = broadcast(column, "col", pivot_index % cols_axis)
        diag_block = lax.dynamic_slice_in_dim(column, pivot_index // rows_axis * BLK, BLK, 0)
        diag_block = broadcast(diag_block, "row", pivot_index % rows_axis)
        diag_factor = jnp.tril(jnp.linalg.cholesky(diag_block))
        solved = lax.linalg.triangular_solve(
            diag_factor, column, left_side=False, lower=True, transpose_a=True
        )
        panel_tiles = solved.reshape(front_rows, BLK, BLK)
        panel_tiles = jnp.where(
            (row_blocks == pivot_index)[:, None, None], diag_factor[None], panel_tiles
        )
        stored_col = jnp.where(
            (row_blocks >= pivot_index)[:, None, None], panel_tiles, 0.0
        ).reshape(front_rows * BLK, BLK)
        below_rows = jnp.where((row_blocks > pivot_index)[:, None, None], panel_tiles, 0.0).reshape(
            front_rows * BLK, BLK
        )
        received = [
            broadcast(below_rows, "row", own_col + offset * cols_axis).reshape(front_rows, BLK, BLK)
            for offset in range(spread)
        ]
        across_cols = jnp.stack(received, axis=1).reshape(front_cols * BLK, BLK)
        updated = current_front - lax.dot_general(
            below_rows,
            across_cols,
            (((1,), (1,)), ((), ())),
            precision=lax.Precision.HIGHEST,
            preferred_element_type=jnp.float32,
        )
        present = lax.dynamic_slice_in_dim(updated, col_slot * BLK, BLK, 1)
        column_new = jnp.where(own_col == pivot_index % cols_axis, stored_col, present)
        return lax.dynamic_update_slice_in_dim(updated, column_new, col_slot * BLK, 1)

    finished = lax.fori_loop(0, SEP // BLK, eliminate, assembled)
    upper_mask = (row_blocks < SEP // BLK)[:, None] & (col_blocks >= SEP // BLK)[None, :]
    finished = finished.reshape(front_rows, BLK, front_cols, BLK)
    finished = jnp.where(upper_mask[:, None, :, None], 0.0, finished)
    return finished.reshape(front_rows * BLK, front_cols * BLK)


def solution(mesh):
    in_specs = (P(("front", "row"), "col"), P("front", "row", "col"), P("front", None))
    out_specs = P(("front", "row"), "col")
    return jax.shard_map(shards, mesh=mesh, in_specs=in_specs, out_specs=out_specs, check_vma=False)
```

profile of v0, /device:TPU:13, one launch (start us, length us, event | category | flops | bytes accessed | tf_op | source)
XLA Modules:
  0.0 779.1 jit_solution(9959633989343557825)
XLA Ops:
  11.7 9.9 %copy.114 = bf16[256,8,16,128]{3,2,1,0:T(8,128)(2,1)} copy(bf16[256,8,16,128]{3,1,2,0:T(8,128)(2,1)} %bitcast.166) | data formatting | bytes 16777216
  47.7 10.5 %copy.98 = bf16[2,8,128,16,128]{4,2,3,1,0:T(8,128)(2,1)} copy(bf16[2,8,128,16,128]{4,2,1,3,0:T(8,128)(2,1)} %bitcast.157) | data formatting | bytes 16777216 | tf_op jit(solution)/shard_map/jit(take_along_axis)/gather | solution.py:47
  66.0 10.5 %copy.99 = bf16[2,32,1,128,4,128]{5,3,4,2,0,1:T(8,128)(2,1)} copy(bf16[2,32,1,128,4,128]{5,3,4,2,1,0:T(8,128)(2,1)} %bitcast.161) | data formatting | bytes 16777216 | tf_op jit(solution)/shard_map/reshape | solution.py:49
  85.3 10.9 %reshape.509 = f32[9,128,18,128]{3,2,1,0:T(8,128)} reshape(bf16[1152,2304]{1,0:T(8,128)(2,1)} %param.5) | data formatting | bytes 15925248 | tf_op jit(solution)/shard_map/reshape | solution.py:58
  96.2 11.0 %copy.100 = f32[9,128,18,128]{3,1,2,0:T(8,128)} copy(f32[9,128,18,128]{3,2,1,0:T(8,128)} %reshape.509) | data formatting | bytes 21233664 | tf_op jit(solution)/shard_map/reshape | solution.py:58
  111.8 68.7 %all-to-all-done = bf16[2,32,1,128,4,128]{5,3,4,2,0,1:T(8,128)(2,1)} async-done(((bf16[2,32,1,128,4,128]{5,3,4,2,0,1:T(8,128)(2,1)}), bf16[2,32,1,128,4,128]{5,3,4,2,0,1:T(8,128)(2,1)}, u32[]{:S(2)}, u32[]{:S(2)}) %all-to-all-start) | async-done | bytes 8388640 | tf_op jit(solution)/shard_map/all_to_all | solution.py:52
  192.9 27.2 %scatter_fusion = f32[9,128,18,128]{3,1,2,0:T(8,128)} fusion(f32[9,128,18,128]{3,1,2,0:T(8,128)} %copy.100, s32[128]{0:T(128)S(1)} %reshape.570, f32[128,128,128]{2,1,0:T(8,128)} %bitcast.155), kind=kCustom, calls=%fused_computation.8 | custom fusion | flops 2097152 | bytes 25166848 | tf_op jit(solution)/shard_map/scatter-add | solution.py:63
  220.1 27.4 %scatter_fusion.1 = f32[9,128,18,128]{3,1,2,0:T(8,128)} fusion(f32[9,128,18,128]{3,1,2,0:T(8,128)} %scatter_fusion, s32[128]{0:T(128)S(1)} %reshape.576, f32[128,128,128]{2,1,0:T(8,128)} %bitcast.156), kind=kCustom, calls=%fused_computation.9 | custom fusion | flops 2097152 | bytes 25166848 | tf_op jit(solution)/shard_map/scatter-add | solution.py:63
  247.5 15.3 %copy.102 = f32[9,128,18,128]{3,2,1,0:T(8,128)} copy(f32[9,128,18,128]{3,1,2,0:T(8,128)} %scatter_fusion.1) | data formatting | bytes 21233664 | tf_op jit(solution)/shard_map/scatter-add | solution.py:63
  262.9 11.7 %copy.119 = f32[144,8,18,128]{3,1,2,0:T(8,128)} copy(f32[144,8,18,128]{3,2,1,0:T(8,128)} %bitcast.154) | data formatting | bytes 21233664
  274.6 486.5 %while.17 = (s32[]{:T(128)}, f32[1152,2304]{1,0:T(8,128)}, s32[]{:T(128)}, s32[]{:T(128)}, s32[]{:T(128)}, /*index=5*/s32[]{:T(128)}, s32[]{:T(128)}, s32[]{:T(1...) while((s32[]{:T(128)}, f32[1152,2304]{1,0:T(8,128)}, ...), condition=%wide.region_13.14_spmd.clone, body=%wide.region_6.13_spmd.clone.sunk | while | flops 4307976192 | bytes 43714316 | solution.py:105
  276.9 43.6 %all-reduce.7.cloned.1.call-done = f32[1152,128]{1,0:T(8,128)} async-done(((f32[1152,128]{1,0:T(8,128)}), f32[1152,128]{1,0:T(8,128)}) %all-reduce.7.cloned.1.call-update) | async-done | bytes 589840 | tf_op jit(solution)/shard_map/while/body/eval_jaxpr/psum | solution.py:12
  322.1 69.9 %all-reduce.9.cloned.1.call-done = f32[128,128]{1,0:T(8,128)} async-done(((f32[128,128]{1,0:T(8,128)}), f32[128,128]{1,0:T(8,128)}) %all-reduce.9.cloned.1.call-update) | async-done | bytes 65552 | tf_op jit(solution)/shard_map/while/body/eval_jaxpr/psum | solution.py:12
  393.8 11.7 %cholesky.64 = f32[128,128]{1,0:T(8,128)S(1)} custom-call(f32[128,128]{1,0:T(8,128)S(1)} %fusion.31), custom_call_target="Cholesky" | custom-call | tf_op jit(solution)/shard_map/while/body/eval_jaxpr/jit(cholesky)/cholesky | solution.py:75
  406.8 9.8 %custom-call.44 = f32[1,128,128]{1,2,0:T(8,128)S(1)} custom-call(f32[1,128,128]{2,1,0:T(8,128)S(1)} %get-tuple-element.255), custom_call_target="InvertDiagBlocksLowerTriangular" | custom-call | tf_op jit(solution)/shard_map/while/body/eval_jaxpr/triangular_solve | solution.py:76
  419.4 81.4 %all-reduce.11.cloned.1.call-done = (f32[9,1,128,128]{3,2,1,0:T(8,128)}, f32[9,1,128,128]{3,2,1,0:T(8,128)}) async-done(((f32[9,1,128,128]{3,2,1,0:T(8,128)}, f32[9,1,128,128]{3,2,1,0:T(8,128)}), (f32[9,1,128,128]{3,2,1,0:T(8,128)}, f32[9,1,128,128]{3,2,1,0:T(8,128)})) %all-reduce.11.cloned.1.call-update) | async-done | bytes 1179664 | tf_op jit(solution)/shard_map/while/body/eval_jaxpr/psum | solution.py:12
  502.1 13.0 %convolution_subtract_fusion.2 = f32[1152,2304]{1,0:T(8,128)} fusion(f32[1152,2304]{1,0:T(8,128)} %get-tuple-element.284, f32[1152,128]{1,0:T(8,128)S(1)} %bitcast.150, f32[2304,128]{1,0:T(8,128)S(1)} %bitcast.151), kind=kOutput, calls=%fused_computation.11.clone.1 | convolution fusion | flops 4079517696 | bytes 23003136 | tf_op jit(solution)/shard_map/while/body/eval_jaxpr/dot_general | solution.py:94
  519.1 45.5 %all-reduce.7.cloned.1.call-done = f32[1152,128]{1,0:T(8,128)} async-done(((f32[1152,128]{1,0:T(8,128)}), f32[1152,128]{1,0:T(8,128)}) %all-reduce.7.cloned.1.call-update) | async-done | bytes 589840 | tf_op jit(solution)/shard_map/while/body/eval_jaxpr/psum | solution.py:12
  566.1 69.8 %all-reduce.9.cloned.1.call-done = f32[128,128]{1,0:T(8,128)} async-done(((f32[128,128]{1,0:T(8,128)}), f32[128,128]{1,0:T(8,128)}) %all-reduce.9.cloned.1.call-update) | async-done | bytes 65552 | tf_op jit(solution)/shard_map/while/body/eval_jaxpr/psum | solution.py:12
  637.7 11.7 %cholesky.64 = f32[128,128]{1,0:T(8,128)S(1)} custom-call(f32[128,128]{1,0:T(8,128)S(1)} %fusion.31), custom_call_target="Cholesky" | custom-call | tf_op jit(solution)/shard_map/while/body/eval_jaxpr/jit(cholesky)/cholesky | solution.py:75
  650.7 9.8 %custom-call.44 = f32[1,128,128]{1,2,0:T(8,128)S(1)} custom-call(f32[1,128,128]{2,1,0:T(8,128)S(1)} %get-tuple-element.255), custom_call_target="InvertDiagBlocksLowerTriangular" | custom-call | tf_op jit(solution)/shard_map/while/body/eval_jaxpr/triangular_solve | solution.py:76
  663.3 81.3 %all-reduce.11.cloned.1.call-done = (f32[9,1,128,128]{3,2,1,0:T(8,128)}, f32[9,1,128,128]{3,2,1,0:T(8,128)}) async-done(((f32[9,1,128,128]{3,2,1,0:T(8,128)}, f32[9,1,128,128]{3,2,1,0:T(8,128)}), (f32[9,1,128,128]{3,2,1,0:T(8,128)}, f32[9,1,128,128]{3,2,1,0:T(8,128)})) %all-reduce.11.cloned.1.call-update) | async-done | bytes 1179664 | tf_op jit(solution)/shard_map/while/body/eval_jaxpr/psum | solution.py:12
  746.0 13.0 %convolution_subtract_fusion.2 = f32[1152,2304]{1,0:T(8,128)} fusion(f32[1152,2304]{1,0:T(8,128)} %get-tuple-element.284, f32[1152,128]{1,0:T(8,128)S(1)} %bitcast.150, f32[2304,128]{1,0:T(8,128)S(1)} %bitcast.151), kind=kOutput, calls=%fused_computation.11.clone.1 | convolution fusion | flops 4079517696 | bytes 23003136 | tf_op jit(solution)/shard_map/while/body/eval_jaxpr/dot_general | solution.py:94
  762.1 9.9 %bitcast_select_fusion.1 = f32[1152,2304]{1,0:T(8,128)} fusion(f32[1152,2304]{1,0:T(8,128)} %get-tuple-element.166, pred[144,8,18,128]{3,2,1,0:T(8,128)(4,1)S(1)} %bitcast.165), kind=kLoop, calls=%fused_computation.36 | loop fusion | flops 2654208 | bytes 23887872 | tf_op jit(solution)/shard_map/jit(_where)/select_n | solution.py:108
  (127 shorter events, 90.9 us)
Async XLA Ops:
  76.5 104.0 %all-to-all-start = ((bf16[2,32,1,128,4,128]{5,3,4,2,0,1:T(8,128)(2,1)}), bf16[2,32,1,128,4,128]{5,3,4,2,0,1:T(8,128)(2,1)}, u32[]{:S(2)}, u32[]{:S(2)}) async-start(bf16[2,32,1,128,4,128]{5,3,4,2,0,1:T(8,128)(2,1)} %copy.99), calls=%async_computation | async-start | bytes 16777216 | tf_op jit(solution)/shard_map/all_to_all | solution.py:52
  274.8 45.7 %all-reduce.7.cloned.1.call-start = ((), (), s32[]{:S(2)}) async-start(), calls=%async_computation.1 | async-start | bytes 1179648 | tf_op jit(solution)/shard_map/while/body/eval_jaxpr/psum | solution.py:12
  276.8 115.2 %all-reduce.9.cloned.1.call-start = ((), (), s32[]{:S(2)}) async-start(), calls=%async_computation.2 | async-start | bytes 131072 | tf_op jit(solution)/shard_map/while/body/eval_jaxpr/psum | solution.py:12
  322.0 178.8 %all-reduce.11.cloned.1.call-start = ((), (), s32[]{:S(2)}) async-start(), calls=%async_computation.3 | async-start | bytes 2359296 | tf_op jit(solution)/shard_map/while/body/eval_jaxpr/psum | solution.py:12
  517.1 47.5 %all-reduce.7.cloned.1.call-start = ((), (), s32[]{:S(2)}) async-start(), calls=%async_computation.1 | async-start | bytes 1179648 | tf_op jit(solution)/shard_map/while/body/eval_jaxpr/psum | solution.py:12
  519.0 116.9 %all-reduce.9.cloned.1.call-start = ((), (), s32[]{:S(2)}) async-start(), calls=%async_computation.2 | async-start | bytes 131072 | tf_op jit(solution)/shard_map/while/body/eval_jaxpr/psum | solution.py:12
  566.1 178.6 %all-reduce.11.cloned.1.call-start = ((), (), s32[]{:S(2)}) async-start(), calls=%async_computation.3 | async-start | bytes 2359296 | tf_op jit(solution)/shard_map/while/body/eval_jaxpr/psum | solution.py:12
Sparse Core Ops, SparseCore 0:
  278.1 42.3 all-reduce.6
  323.0 68.9 all-reduce.8
  419.5 81.2 all-reduce.10
  520.1 44.4 all-reduce.6
  566.9 68.9 all-reduce.8
  663.5 81.1 all-reduce.10
where the time goes:
time: 794 us; the launch traced here: 779 us
  waiting for transfers between devices  460 us (58%)
  other arithmetic  156 us (20%)
  local copies, waits for them, and re-layouts  110 us (14%)
  matrix products  29.3 us (4%)
  between operations  13.9 us (2%)
  starting transfers between devices  9.01 us (1%)
    psum x6, waiting for transfers between devices, broadcast(): return lax.psum(kept, axis)  392 us
    all_to_all x1, waiting for transfers between devices, shards(): lax.all_to_all(outgoing, ('row', 'col'), split_axis=1, concat_axis=1, til...  68.7 us
    scatter-add x2, other arithmetic, shards(): assembled = assembled.at[row_dest[child_index][:, None], :, col_dest[chil...  54.6 us
    dot_general x2, matrix products, eliminate(): lax.dot_general(below_rows, across_cols, (((1,), (1,)), ((), ())), precis...  26 us
    another operation x6, other arithmetic, eliminate(): diag_factor = jnp.tril(jnp.linalg.cholesky(diag_block))  24.8 us
    unnamed x5, local copies, waits for them, and re-layouts  22.4 us
    reshape x2, local copies, waits for them, and re-layouts, shards(): front_entries.astype(jnp.float32).reshape(front_rows, BLK, front_cols, BLK)  21.8 us
    another operation x4, other arithmetic, eliminate(): lax.linalg.triangular_solve(diag_factor, column, left_side=False, lower=T...  20.8 us
  transfers between devices with their start and end apart: 7, of which 7 were waited for; matrix products, arithmetic and copies ran while one was open for 3% of the time, Pallas kernels for 0%

commit v1 on v0

v1 whole, which is shorter than its diff:
```python
import jax
import jax.numpy as jnp
from jax import lax
from jax.experimental import pallas as pl
from jax.experimental.pallas import tpu as pltpu
from jax.sharding import PartitionSpec as P

BLK = 128
F32 = jnp.float32
BF16 = jnp.bfloat16
HIGH = lax.Precision.HIGHEST


def pack_kernel(maps, pos, children, out, buf, packed, row_of, col_of, in_sem, out_sem):
    own_row, own_col = pos[0], pos[1]
    for c in range(2):
        for k in range(8):
            row_of[c, maps[c, k * 8 + own_row] % 8] = k
        for k in range(16):
            col_of[c, (k % 2) * 8 + maps[c, k * 4 + own_col] % 8] = k
    for d in range(8):
        for c in range(2):
            pltpu.make_async_copy(
                children.at[c, pl.ds(row_of[c, d] * BLK, BLK), :], buf.at[d, c], in_sem.at[d]
            ).start()

    def one_row(d, carry):
        for c in range(2):
            pltpu.make_async_copy(children.at[0, pl.ds(0, BLK), :], buf.at[d, c], in_sem.at[d]).wait()
        for c in range(2):
            for half in range(2):
                for delta in range(8):
                    start = pl.multiple_of(col_of[c, half * 8 + delta] * BLK, BLK)
                    packed[d, delta % 4, half, delta // 4, c] = buf[d, c, :, pl.ds(start, BLK)]
        pltpu.make_async_copy(packed.at[d], out.at[d], out_sem.at[0]).start()
        return carry

    lax.fori_loop(0, 8, one_row, 0)
    pltpu.make_async_copy(packed, out, out_sem.at[0]).wait()


def pack(children, child_maps, pos):
    return pl.pallas_call(
        pack_kernel,
        out_shape=jax.ShapeDtypeStruct((8, 4, 2, 2, 2, BLK, BLK), BF16),
        in_specs=[
            pl.BlockSpec(memory_space=pltpu.SMEM),
            pl.BlockSpec(memory_space=pltpu.SMEM),
            pl.BlockSpec(memory_space=pl.ANY),
        ],
        out_specs=pl.BlockSpec(memory_space=pl.ANY),
        scratch_shapes=[
            pltpu.VMEM((8, 2, BLK, 16 * BLK), BF16),
            pltpu.VMEM((8, 4, 2, 2, 2, BLK, BLK), BF16),
            pltpu.SMEM((2, 8), jnp.int32),
            pltpu.SMEM((2, 16), jnp.int32),
            pltpu.SemaphoreType.DMA((8,)),
            pltpu.SemaphoreType.DMA((1,)),
        ],
        compiler_params=pltpu.CompilerParams(vmem_limit_bytes=40 << 20),
        name="pack",
    )(child_maps, pos, children)


def slot_tables(child_maps, own_row, own_col):
    ids = jnp.arange(64, dtype=jnp.int32)
    rows = jnp.arange(9, dtype=jnp.int32) * 8 + own_row
    cols = jnp.arange(18, dtype=jnp.int32) * 4 + own_col
    unit = ids % 4 * 2 + ids % 8 // 4
    row_tab = jnp.max(jnp.where(child_maps[:, None, :] == rows[None, :, None], ids % 8, -1), axis=2)
    col_tab = jnp.max(jnp.where(child_maps[:, None, :] == cols[None, :, None], unit, -1), axis=2)
    return jnp.concatenate([row_tab, col_tab], axis=1).astype(jnp.int32)


def panel_kernel(tab, recv, front, out, acc, sem):
    out[...] = front[...].astype(F32)
    for c in range(2):
        col = tab[c, 9]
        for s in range(9):
            row = tab[c, s]

            @pl.when((row >= 0) & (col >= 0))
            def _():
                copy = pltpu.make_async_copy(recv.at[row, col, 0, c], acc, sem)
                copy.start()
                copy.wait()
                out[pl.ds(s * BLK, BLK), :] += acc[...].astype(F32)


def panel(recv, front, tab):
    return pl.pallas_call(
        panel_kernel,
        out_shape=jax.ShapeDtypeStruct((9 * BLK, BLK), F32),
        grid=(1,),
        in_specs=[
            pl.BlockSpec(memory_space=pltpu.SMEM),
            pl.BlockSpec(memory_space=pl.ANY),
            pl.BlockSpec((9 * BLK, BLK), lambda i: (0, 0)),
        ],
        out_specs=pl.BlockSpec((9 * BLK, BLK), lambda i: (0, 0)),
        scratch_shapes=[pltpu.VMEM((BLK, BLK), BF16), pltpu.SemaphoreType.DMA(())],
        name="panel",
    )(tab, recv, front)


def split(x):
    hi = x.astype(BF16)
    lo = (x - hi.astype(F32)).astype(BF16)
    return hi, lo


def final_kernel(tab, pos, recv0, recv1, front, rows, cols, out, colcat):
    s = pl.program_id(0)
    own_row, own_col = pos[0], pos[1]

    @pl.when(s == 0)
    def _():
        hi, lo = split(cols[...])
        colcat[:, pl.ds(0, 256)] = hi
        colcat[:, pl.ds(256, 256)] = lo

    lead = (s == 0) & (own_row < 2)

    @pl.when(lead)
    def _():
        out[...] = jnp.zeros_like(out)

        @pl.when(own_col < 2)
        def _():
            r = lax.broadcasted_iota(jnp.int32, (BLK, BLK), 0) + own_row * BLK
            k = lax.broadcasted_iota(jnp.int32, (BLK, BLK), 1) + own_col * BLK
            mine = jnp.where(own_col == 0, rows[:, pl.ds(0, BLK)], rows[:, pl.ds(BLK, BLK)])
            out[:, pl.ds(0, BLK)] = jnp.where(r >= k, mine, 0.0)

    @pl.when(jnp.logical_not(lead))
    def _():
        hi, lo = split(rows[...])
        left = jnp.concatenate([hi, lo, hi], axis=1)
        for t in range(18):
            part = pl.ds(t * BLK, BLK)
            right = jnp.concatenate(
                [colcat[part, pl.ds(0, 256)], colcat[part, pl.ds(0, 256)], colcat[part, pl.ds(256, 256)]], axis=1
            )
            val = front[:, part].astype(F32) - lax.dot_general(
                left, right, (((1,), (1,)), ((), ())), preferred_element_type=F32
            )
            for c, recv in enumerate((recv0, recv1)):
                u = tab[c, 9 + t]
                ok = (u >= 0) & (tab[c, s] >= 0)
                blk = recv[0, jnp.maximum(u, 0), t % 2, 0].astype(F32)
                val += jnp.where(ok, blk, 0.0)
            out[:, part] = val

        @pl.when(own_col < 2)
        def _():
            out[:, pl.ds(0, BLK)] = jnp.where(own_col == 0, rows[:, pl.ds(0, BLK)], rows[:, pl.ds(BLK, BLK)])


def final(tab, pos, recv, front, rows, cols):
    def recv_spec(c):
        return pl.BlockSpec(
            (1, 8, 2, 1, BLK, BLK), lambda s, tab, pos: (jnp.maximum(tab[c, s], 0), 0, 0, c, 0, 0)
        )

    return pl.pallas_call(
        final_kernel,
        out_shape=jax.ShapeDtypeStruct((9 * BLK, 18 * BLK), F32),
        grid_spec=pltpu.PrefetchScalarGridSpec(
            num_scalar_prefetch=2,
            grid=(9,),
            in_specs=[
                recv_spec(0),
                recv_spec(1),
                pl.BlockSpec((BLK, 18 * BLK), lambda s, *_: (s, 0)),
                pl.BlockSpec((BLK, 2 * BLK), lambda s, *_: (s, 0)),
                pl.BlockSpec((18 * BLK, 2 * BLK), lambda s, *_: (0, 0)),
            ],
            out_specs=pl.BlockSpec((BLK, 18 * BLK), lambda s, *_: (s, 0)),
            scratch_shapes=[pltpu.VMEM((18 * BLK, 4 * BLK), BF16)],
        ),
        compiler_params=pltpu.CompilerParams(vmem_limit_bytes=40 << 20),
        name="final",
    )(tab, pos, recv, recv, front, rows, cols)


def shards(front_entries, children, child_maps):
    own_row = lax.axis_index("row")
    own_col = lax.axis_index("col")
    pos = jnp.stack([own_row, own_col]).astype(jnp.int32)
    packed = pack(children, child_maps, pos).reshape(32, 8, BLK, BLK)
    recv = lax.all_to_all(packed, ("row", "col"), split_axis=0, concat_axis=0, tiled=True)
    recv = recv.reshape(8, 8, 2, 2, BLK, BLK)
    tab = slot_tables(child_maps, own_row, own_col)
    mine = panel(recv, front_entries, tab)
    both = lax.psum(jnp.stack([jnp.where(own_col == p, mine, 0.0) for p in range(2)]), "col")
    rows = both.transpose(1, 0, 2).reshape(9 * BLK, 2 * BLK)
    every = lax.all_gather(rows.reshape(9, BLK, 2 * BLK), "row", axis=0)
    corner = every[:2, 0].reshape(2 * BLK, 2 * BLK)
    low = jnp.tril(jnp.linalg.cholesky(corner))
    inv = lax.linalg.triangular_solve(low, jnp.eye(2 * BLK, dtype=F32), left_side=True, lower=True)
    picked = jnp.stack([lax.dynamic_index_in_dim(every, own_col + 4 * h, 0, False) for h in range(2)], axis=1)
    cols = picked.reshape(18 * BLK, 2 * BLK)
    dims = (((1,), (1,)), ((), ()))
    rows = lax.dot_general(rows, inv, dims, precision=HIGH, preferred_element_type=F32)
    cols = lax.dot_general(cols, inv, dims, precision=HIGH, preferred_element_type=F32)
    return final(tab, pos, recv, front_entries, rows, cols)


def solution(mesh):
    in_specs = (P(("front", "row"), "col"), P("front", "row", "col"), P("front", None))
    out_specs = P(("front", "row"), "col")
    return jax.shard_map(shards, mesh=mesh, in_specs=in_specs, out_specs=out_specs, check_vma=False)
```

time: 794 us -> 472 us (0.59); the launches traced: 779 us -> 468 us
  waiting for transfers between devices: 460 us -> 334 us
  other arithmetic: 156 us -> 58.5 us
  local copies, waits for them, and re-layouts: 110 us -> 19.5 us
  Pallas kernels: 0 us -> 27.4 us
  matrix products: 29.3 us -> 5.54 us
    psum x6 -> x1, waiting for transfers between devices: 392 us -> 52.9 us  [shards(): lax.psum(jnp.stack([jnp.where(own_col == p, mine, 0.0) for p in range(2)]...]
    all_gather x0 -> x1, waiting for transfers between devices: none -> 187 us  [shards(): every = lax.all_gather(rows.reshape(9, BLK, 2 * BLK), 'row', axis=0)]
    scatter-add x2 -> x0, other arithmetic: 54.6 us -> none  [shards(): assembled = assembled.at[row_dest[child_index][:, None], :, col_dest[chil...]
    select_n x16 -> x1, other arithmetic: 35.5 us -> 0.01 us  [slot_tables(): ids % 8]
    reshape x3 -> x0, local copies, waits for them, and re-layouts: 32.3 us -> none  [the longest x2 21.8 us: shards(): front_entries.astype(jnp.float32).reshape(front_rows, BLK, front_cols, BLK)]
    gather x22 -> x0, local copies, waits for them, and re-layouts: 32.2 us -> none  [the longest x4 19.3 us: shards(): jnp.take_along_axis(tile_grid, col_order[:, None, None, :, None], axis=3)]
    pallas_call x0 -> x3, Pallas kernels: none -> 27.4 us  [the longest x1 14.4 us: final(): pl.pallas_call(final_kernel, out_shape=jax.ShapeDtypeStruct((9 * BLK, 18...]
    all_to_all x1, waiting for transfers between devices: 68.7 us -> 93.5 us  [shards(): lax.all_to_all(packed, ('row', 'col'), split_axis=0, concat_axis=0, tiled...]
  transfers between devices with their start and end apart: 7 -> 3, of which waited for: 7 -> 3; matrix products, arithmetic and copies ran while one was open for 3% -> 0% of each run, Pallas kernels for 0% -> 0%
where the time goes in v1:
time: 472 us; the launch traced here: 468 us
  waiting for transfers between devices  334 us (71%)
  other arithmetic  58.5 us (12%)
  Pallas kernels  27.4 us (6%)
  local copies, waits for them, and re-layouts  19.5 us (4%)
  between operations  14.9 us (3%)
  starting transfers between devices  9.02 us (2%)
  matrix products  5.54 us (1%)
    all_gather x1, waiting for transfers between devices, shards(): every = lax.all_gather(rows.reshape(9, BLK, 2 * BLK), 'row', axis=0)  187 us
    all_to_all x1, waiting for transfers between devices, shards(): lax.all_to_all(packed, ('row', 'col'), split_axis=0, concat_axis=0, tiled...  93.5 us
    psum x1, waiting for transfers between devices, shards(): lax.psum(jnp.stack([jnp.where(own_col == p, mine, 0.0) for p in range(2)]...  52.9 us
    another operation x7, other arithmetic, shards(): low = jnp.tril(jnp.linalg.cholesky(corner))  34.6 us
    another operation x3, other arithmetic, shards(): lax.linalg.triangular_solve(low, jnp.eye(2 * BLK, dtype=F32), left_side=T...  19.9 us
    pallas_call x1, Pallas kernels, final(): pl.pallas_call(final_kernel, out_shape=jax.ShapeDtypeStruct((9 * BLK, 18...  14.4 us
  transfers between devices with their start and end apart: 3, of which 3 were waited for; matrix products, arithmetic and copies ran while one was open for 0% of the time, Pallas kernels for 0%

profile of v1, /device:TPU:13, one launch (start us, length us, event | category | flops | bytes accessed | tf_op | source)
XLA Modules:
  0.0 468.5 jit_solution(5112809153798046656)
XLA Ops:
  7.3 5.0 %pack.1 = bf16[8,4,2,2,2,128,128]{6,5,4,3,2,1,0:T(8,128)(2,1)S(1)} custom-call(s32[2,64]{1,0:T(2,128)S(1)} %copy-done.2, s32[2]{0:T(128)S(1)} %pad_add_fusion.1.pos, bf16[2,1024,2048]{2,1,0:T(8,128)(2,1)} %children.1), custom_call_target="tpu_custom_call" | custom-call | tf_op jit(solution)/shard_map/pack/pallas_call | solution.py:43
  12.3 3.4 copy-done
  15.7 8.9 %all-to-all-start = ((bf16[32,8,128,128]{3,2,1,0:T(8,128)(2,1)}), bf16[32,8,128,128]{3,2,1,0:T(8,128)(2,1)}, u32[]{:S(2)}, u32[]{:S(2)}) async-start(bf16[32,8,128,128]{3,2,1,0:T(8,128)(2,1)} %bitcast.51), calls=%async_computation | async-start | bytes 16777216 | tf_op jit(solution)/shard_map/all_to_all | solution.py:191
  26.3 93.5 %all-to-all-done = bf16[32,8,128,128]{3,2,1,0:T(8,128)(2,1)} async-done(((bf16[32,8,128,128]{3,2,1,0:T(8,128)(2,1)}), bf16[32,8,128,128]{3,2,1,0:T(8,128)(2,1)}, u32[]{:S(2)}, u32[]{:S(2)}) %all-to-all-start) | async-done | bytes 8388640 | tf_op jit(solution)/shard_map/all_to_all | solution.py:191
  119.8 8.0 %panel.1 = f32[1152,128]{1,0:T(8,128)} custom-call(s32[2,27]{1,0:T(2,128)} %pad_add_fusion.tab, bf16[8,8,2,2,128,128]{5,4,3,2,1,0:T(8,128)(2,1)} %bitcast.3.recv.recv0.recv1, bf16[1152,2304]{1,0:T(8,128)(2,1)} %front.3), custom_call_target="tpu_custom_call" | custom-call | tf_op jit(solution)/shard_map/panel/pallas_call | solution.py:91
  127.9 1.1 select_bitcast_fusion.1
  129.0 1.1 maximum_bitcast_fusion
  130.2 52.9 %all-reduce.3.cloned.1.call-done = f32[1152,2,128]{2,0,1:T(8,128)} async-done(((f32[1152,2,128]{2,0,1:T(8,128)}), f32[1152,2,128]{2,0,1:T(8,128)}) %all-reduce.3.cloned.1.call-update) | async-done | bytes 1179664 | tf_op jit(solution)/shard_map/psum | solution.py:195
  183.1 4.9 %copy.16 = f32[1152,2,128]{2,1,0:T(2,128)S(1)} copy(f32[1152,2,128]{2,0,1:T(8,128)} %all-reduce.3.cloned.1.call-done) | data formatting | bytes 2359296 | tf_op jit(solution)/shard_map/psum | solution.py:195
  188.0 2.0 all_gather_reshape_reshape.3
  190.1 1.2 copy-done.4
  191.6 187.1 %all-gather.2.cloned.1.call-done = f32[8,9,128,256]{3,2,1,0:T(8,128)} async-done(((f32[1,9,128,256]{3,2,1,0:T(8,128)}), f32[8,9,128,256]{3,2,1,0:T(8,128)}) %all-gather.2.cloned.1.call-update) | async-done | bytes 9437200 | tf_op jit(solution)/shard_map/all_gather | solution.py:197
  378.7 1.0 slice.58
  379.9 11.7 %cholesky.50 = f32[128,128]{1,0:T(8,128)S(1)} custom-call(f32[128,128]{1,0:T(8,128)S(1)} %cholesky.118), custom_call_target="Cholesky" | custom-call | tf_op jit(solution)/shard_map/jit(cholesky)/cholesky | solution.py:199
  392.3 9.8 %custom-call.14 = f32[1,128,128]{1,2,0:T(8,128)S(1)} custom-call(f32[1,128,128]{2,1,0:T(8,128)S(1)} %get-tuple-element.30), custom_call_target="InvertDiagBlocksLowerTriangular" | custom-call | tf_op jit(solution)/shard_map/jit(cholesky)/cholesky | solution.py:199
  402.6 11.7 %cholesky.105 = f32[128,128]{1,0:T(8,128)S(1)} custom-call(f32[128,128]{1,0:T(8,128)S(1)} %convolution_subtract_fusion.1), custom_call_target="Cholesky" | custom-call | tf_op jit(solution)/shard_map/jit(cholesky)/cholesky | solution.py:199
  416.3 3.8 while.1
  416.9 1.3 bitcast_dynamic-update-slice_fusion.2
  418.8 1.3 bitcast_dynamic-update-slice_fusion.2
  420.1 19.9 %custom-call.15 = f32[2,128,128]{1,2,0:T(8,128)S(1)} custom-call(f32[2,128,128]{2,1,0:T(8,128)S(1)} %get-tuple-element.12), custom_call_target="InvertDiagBlocksLowerTriangular" | custom-call | tf_op jit(solution)/shard_map/triangular_solve | solution.py:200
  440.9 1.8 dynamic-slice_bitcast_fusion.1
  442.9 2.2 fusion.1.cols
  445.1 2.1 fusion.2.rows
  447.2 14.4 %final.1 = f32[1152,2304]{1,0:T(8,128)} custom-call(s32[2,27]{1,0:T(2,128)S(1)} %copy-done.1, s32[2]{0:T(128)S(1)} %pad_add_fusion.1.pos, bf16[8,8,2,2,128,128]{5,4,3,2,1,0:T(8,128)(2,1)} %bitcast.3.recv.recv0.recv1, bf16[8,8,2,2,128,128]{5,4,3,2,1,0:T(8,128)(2,1)} %bitcast.3.recv.recv0.recv1, bf16[1152,2304]{1,0:T(8,128)(2,1)S(1)} %bitcast.53, ...), custom_call_target="tpu_custom_call" | custom-call | tf_op jit(solution)/shard_map/final/pallas_call | solution.py:165
  (50 shorter events, 7.2 us)
Async XLA Ops:
  6.6 0.7 copy-start.2
  12.3 3.4 copy-start
  15.7 9.0 %copy-start.3 = (s32[2,64]{1,0:T(2,128)S(1)}, s32[2,64]{1,0:T(2,128)}, u32[]{:S(2)}) copy-start(s32[2,64]{1,0:T(2,128)} %maps.1) | copy-start | bytes 1540
  15.7 104.1 %all-to-all-start = ((bf16[32,8,128,128]{3,2,1,0:T(8,128)(2,1)}), bf16[32,8,128,128]{3,2,1,0:T(8,128)(2,1)}, u32[]{:S(2)}, u32[]{:S(2)}) async-start(bf16[32,8,128,128]{3,2,1,0:T(8,128)(2,1)} %bitcast.51), calls=%async_computation | async-start | bytes 16777216 | tf_op jit(solution)/shard_map/all_to_all | solution.py:191
  24.6 158.5 %all-reduce.3.cloned.1.call-start = ((), (), s32[]{:S(2)}) async-start(), calls=%async_computation.1 | async-start | bytes 2359296 | tf_op jit(solution)/shard_map/psum | solution.py:195
  130.1 248.6 %all-gather.2.cloned.1.call-start = ((), (), s32[]{:S(2)}) async-start(), calls=%async_computation.2 | async-start | bytes 10616832 | tf_op jit(solution)/shard_map/all_gather | solution.py:197
  190.0 1.3 copy-start.4
  442.7 4.5 slice-start
  442.9 4.3 slice-start.1
  445.1 2.1 copy-start.1
Sparse Core Ops, SparseCore 0:
  130.2 52.8 all-reduce.2
  190.1 188.5 all-gather.1

commit v2 on v1

v2 whole, which is shorter than its diff:
```python
import jax
import jax.numpy as jnp
from jax import lax
from jax.experimental import pallas as pl
from jax.experimental.pallas import tpu as pltpu
from jax.sharding import PartitionSpec as P

BLK = 128
F32 = jnp.float32
BF16 = jnp.bfloat16
HIGH = lax.Precision.HIGHEST


def pack_kernel(maps, pos, children, out, buf, packed, row_of, col_of, in_sem, out_sem):
    own_row, own_col = pos[0], pos[1]
    for c in range(2):
        for k in range(8):
            row_of[c, maps[c, k * 8 + own_row] % 8] = k
        for k in range(16):
            col_of[c, (k % 2) * 8 + maps[c, k * 4 + own_col] % 8] = k
    for d in range(8):
        for c in range(2):
            pltpu.make_async_copy(
                children.at[c, pl.ds(row_of[c, d] * BLK, BLK), :], buf.at[d, c], in_sem.at[d]
            ).start()

    def one_row(d, carry):
        for c in range(2):
            pltpu.make_async_copy(children.at[0, pl.ds(0, BLK), :], buf.at[d, c], in_sem.at[d]).wait()
        for c in range(2):
            for half in range(2):
                for delta in range(8):
                    start = pl.multiple_of(col_of[c, half * 8 + delta] * BLK, BLK)
                    packed[half, d % 4, delta % 4, d // 4, delta // 4, c] = buf[d, c, :, pl.ds(start, BLK)]
        pltpu.make_async_copy(
            packed.at[:, d % 4, :, d // 4], out.at[:, d % 4, :, d // 4], out_sem.at[0]
        ).start()
        return carry

    lax.fori_loop(0, 8, one_row, 0)
    pltpu.make_async_copy(packed, out, out_sem.at[0]).wait()


def pack(children, child_maps, pos):
    return pl.pallas_call(
        pack_kernel,
        out_shape=jax.ShapeDtypeStruct((2, 4, 4, 2, 2, 2, BLK, BLK), BF16),
        in_specs=[
            pl.BlockSpec(memory_space=pltpu.SMEM),
            pl.BlockSpec(memory_space=pltpu.SMEM),
            pl.BlockSpec(memory_space=pl.ANY),
        ],
        out_specs=pl.BlockSpec(memory_space=pl.ANY),
        scratch_shapes=[
            pltpu.VMEM((8, 2, BLK, 16 * BLK), BF16),
            pltpu.VMEM((2, 4, 4, 2, 2, 2, BLK, BLK), BF16),
            pltpu.SMEM((2, 8), jnp.int32),
            pltpu.SMEM((2, 16), jnp.int32),
            pltpu.SemaphoreType.DMA((8,)),
            pltpu.SemaphoreType.DMA((1,)),
        ],
        compiler_params=pltpu.CompilerParams(vmem_limit_bytes=40 << 20),
        name="pack",
    )(child_maps, pos, children)


def identity():
    r = lax.broadcasted_iota(jnp.int32, (BLK, BLK), 0)
    k = lax.broadcasted_iota(jnp.int32, (BLK, BLK), 1)
    return jnp.where(r == k, 1.0, 0.0).astype(BF16)


def place(row, col):
    return col // 2 * 2 + row % 2, row // 2, col % 2


def device(x, z, core):
    return {"row": z * 2 + x % 2, "col": x // 2 * 2 + core}


def ring(t):
    t = (t + 4) % 4
    return t - 2 * (t // 3)


def apart(x, z, tx, tz):
    return ring(tx - x) + ring(tz - z)


def wants(x, z, core, tx, tz, half):
    a, b = z * 2 + x % 2, x // 2 * 2 + core
    alpha = b + 4 * half
    ox, oz, _ = place(alpha, a % 4)
    here, there = apart(x, z, tx, tz), apart(ox, oz, tx, tz)
    return here <= there, here < there


def unit(packed, x, z, core, tx, tz, tcore, half, kind):
    a, b = z * 2 + x % 2, x // 2 * 2 + core
    alpha = b + 4 * half
    d, e = tz * 2 + tx % 2, tx // 2 * 2 + tcore
    if kind == 0:
        return packed.at[half, d % 4, e, d // 4], a * 8 + b * 2 + half
    return packed.at[half, e, d % 4, :, d // 4], alpha * 8 + a % 4 * 2 + a // 4


def far_step(n):
    k = n % 3
    return 2 - k + 3 * (k // 2), 1 + n // 6, n // 3 % 2


def near_step(n):
    dx = (1 - n // 6) * (1 - n // 12) * (n // 2 + 1)
    dz = n // 6 * (1 - n // 12) * ((n - 6) // 2 + 1)
    return dx, dz, n % 2 * (1 - n // 12) + n // 12


def greet_neighbours(barrier, x, z, core):
    def greet(n, carry):
        dx, dz, dc = near_step(n)
        pl.semaphore_signal(
            barrier, inc=1, device_id=device((x + dx) % 4, (z + dz) % 4, (core + dc) % 2),
            device_id_type=pl.DeviceIdType.MESH,
        )
        return carry

    lax.fori_loop(0, 13, greet, 0)
    pl.semaphore_wait(barrier, 13)


def exchange_kernel(packed, recv, hold, send_sem, recv_sem, hold_sem):
    x, z, core = place(lax.axis_index("row"), lax.axis_index("col"))
    barrier = pltpu.get_barrier_semaphore()

    greet_neighbours(barrier, x, z, core)

    def remote(src, dst, arrived, tx, tz, tcore):
        return pltpu.make_async_remote_copy(
            src_ref=src, dst_ref=dst, send_sem=send_sem, recv_sem=arrived,
            device_id=device(tx, tz, tcore), device_id_type=pl.DeviceIdType.MESH,
        )

    def far(n, act):
        dz, dx, dc = far_step(n)
        tx, tz, tcore = (x + dx) % 4, (z + dz) % 4, (core + dc) % 2
        for half in range(2):
            for kind, wanted in enumerate(wants(x, z, core, tx, tz, half)):
                src, _ = unit(packed, x, z, core, tx, tz, tcore, half, kind)
                slot = n * 4 + half * 2 + kind

                @pl.when(wanted)
                def _():
                    act(remote(src, hold.at[slot], hold_sem.at[slot], x, tz, core))

    def near(n, act):
        dx, dz, dc = near_step(n)
        tx, tz, tcore = (x + dx) % 4, (z + dz) % 4, (core + dc) % 2
        for half in range(2):
            for kind, wanted in enumerate(wants(x, z, core, tx, tz, half)):
                src, dst = unit(packed, x, z, core, tx, tz, tcore, half, kind)

                @pl.when(wanted)
                def _():
                    act(remote(src, recv.at[dst], recv_sem.at[dst], tx, tz, tcore))

    def start(n, carry):
        far(n, lambda copy: copy.start())

        @pl.when(n < 13)
        def _():
            near(n, lambda copy: copy.start())

        return carry

    lax.fori_loop(0, 18, start, 0)
    own = [wants(x, z, core, x, z, half) for half in range(2)]
    for half in range(2):
        for kind in range(2):
            src, dst = unit(packed, x, z, core, x, z, core, half, kind)

            @pl.when(own[half][kind])
            def _():
                pltpu.make_async_copy(src, recv.at[dst], recv_sem.at[dst]).start()

    def pass_on(n, act):
        dz, dx, dc = far_step(n)
        sz = (z - dz + 4) % 4
        tx, tcore = (x + dx) % 4, (core + dc) % 2
        for half in range(2):
            for kind, wanted in enumerate(wants(x, sz, core, tx, z, half)):
                _, dst = unit(packed, x, sz, core, tx, z, tcore, half, kind)
                slot = n * 4 + half * 2 + kind

                @pl.when(wanted)
                def _():
                    act(slot, remote(hold.at[slot], recv.at[dst], recv_sem.at[dst], tx, z, tcore))

    def forward(slot, copy):
        pltpu.make_async_copy(hold.at[slot], hold.at[slot], hold_sem.at[slot]).wait()
        copy.start()

    def relay(n, carry):
        pass_on(n, forward)
        return carry

    lax.fori_loop(0, 18, relay, 0)

    def finish(n, carry):
        far(n, lambda copy: copy.wait_send())
        pass_on(n, lambda slot, copy: copy.wait_send())

        @pl.when(n < 13)
        def _():
            near(n, lambda copy: copy.wait_send())

        return carry

    def settle(slot, carry):
        pltpu.make_async_copy(recv.at[slot], recv.at[slot], recv_sem.at[slot]).wait()
        row, u = slot // 8, slot % 8
        alpha = u // 2 + u % 2 * 4
        nx, nz, _ = place(row, alpha % 4)
        ox, oz, _ = place(alpha, row % 4)

        @pl.when(apart(ox, oz, x, z) < apart(nx, nz, x, z))
        def _():
            for h in range(2):
                for c in range(2):
                    recv[slot, h, c] = lax.dot_general(
                        identity(), recv[slot, h, c], (((1,), (1,)), ((), ())), preferred_element_type=F32
                    ).astype(BF16)

        return carry

    lax.fori_loop(0, 64, settle, 0)
    lax.fori_loop(0, 18, finish, 0)


def exchange(packed):
    return pl.pallas_call(
        exchange_kernel,
        out_shape=jax.ShapeDtypeStruct((64, 2, 2, BLK, BLK), BF16),
        in_specs=[pl.BlockSpec(memory_space=pl.ANY)],
        out_specs=pl.BlockSpec(memory_space=pltpu.VMEM),
        scratch_shapes=[
            pltpu.VMEM((72, 2, 2, BLK, BLK), BF16),
            pltpu.SemaphoreType.DMA(()),
            pltpu.SemaphoreType.DMA((64,)),
            pltpu.SemaphoreType.DMA((72,)),
        ],
        compiler_params=pltpu.CompilerParams(
            collective_id=0, has_side_effects=True, vmem_limit_bytes=40 << 20
        ),
        name="exchange",
    )(packed)


def slot_tables(child_maps, own_row, own_col):
    ids = jnp.arange(64, dtype=jnp.int32)
    rows = jnp.arange(9, dtype=jnp.int32) * 8 + own_row
    cols = jnp.arange(18, dtype=jnp.int32) * 4 + own_col
    unit = ids % 4 * 2 + ids % 8 // 4
    row_tab = jnp.max(jnp.where(child_maps[:, None, :] == rows[None, :, None], ids % 8, -1), axis=2)
    col_tab = jnp.max(jnp.where(child_maps[:, None, :] == cols[None, :, None], unit, -1), axis=2)
    a, u = row_tab[:, :, None], col_tab[:, None, :]
    code = jnp.where((a >= 0) & (u >= 0), u, -1)
    return jnp.maximum(row_tab, 0).astype(jnp.int32), code.astype(jnp.int32)


def panel_kernel(tab, code, recv, front, out, acc, sem):
    for s in range(9):
        out[s] = front[pl.ds(s * BLK, BLK), :].astype(F32)
    for c in range(2):
        for s in range(9):
            copy = pltpu.make_async_copy(
                recv.at[tab[c, s] * 8 + jnp.maximum(code[c, s, 0], 0) % 8, 0, c], acc.at[c * 9 + s], sem.at[c * 9 + s]
            )
            copy.start()
    for c in range(2):
        for s in range(9):
            pltpu.make_async_copy(recv.at[0, 0, 0], acc.at[c * 9 + s], sem.at[c * 9 + s]).wait()
            out[s] += jnp.where(code[c, s, 0] >= 0, acc[c * 9 + s].astype(F32), 0.0)


def panel(recv, front, tab, code):
    return pl.pallas_call(
        panel_kernel,
        out_shape=jax.ShapeDtypeStruct((9, BLK, BLK), F32),
        grid=(1,),
        in_specs=[
            pl.BlockSpec(memory_space=pltpu.SMEM),
            pl.BlockSpec(memory_space=pltpu.SMEM),
            pl.BlockSpec(memory_space=pl.ANY),
            pl.BlockSpec((9 * BLK, BLK), lambda i: (0, 0)),
        ],
        out_specs=pl.BlockSpec((9, BLK, BLK), lambda i: (0, 0, 0)),
        scratch_shapes=[pltpu.VMEM((18, BLK, BLK), BF16), pltpu.SemaphoreType.DMA((18,))],
        name="panel",
    )(tab, code, recv, front)


def split(x):
    hi = x.astype(BF16)
    lo = (x - hi.astype(F32)).astype(BF16)
    return hi, lo


def factor_rows(r, mat):
    lane = lax.broadcasted_iota(jnp.int32, (8, 2 * BLK), 1)
    wide = lax.broadcasted_iota(jnp.int32, (8, 4 * BLK), 1)
    sub = lax.broadcasted_iota(jnp.int32, (8, 1), 0)
    rows = pl.ds(pl.multiple_of(r * 8, 8), 8)
    w = mat[rows, :]
    head = w[:, : 2 * BLK]
    col = [jnp.sum(jnp.where(lane == r * 8 + j, head, 0.0), axis=1, keepdims=True) for j in range(8)]
    for j in range(8):
        pivot = col[j][j : j + 1]
        inv = lax.rsqrt(pivot)
        inv = inv * (1.5 - 0.5 * pivot * inv * inv)
        mult = jnp.where(sub > j, col[j] * inv, 0.0)
        for k in range(j + 1, 8):
            col[k] = col[k] - mult * (col[k][j : j + 1] * inv)
        top = w[j : j + 1] * inv
        w = jnp.where(sub == j, top, w - mult * top)
    w = jnp.where(wide < r * 8 + sub, 0.0, w)
    mat[rows, :] = w
    u = w[:, : 2 * BLK]
    update = lax.dot_general(u, w, (((0,), (0,)), ((), ())), precision=HIGH, preferred_element_type=F32)
    below = lax.broadcasted_iota(jnp.int32, (2 * BLK, 1), 0) >= (r + 1) * 8
    mat[...] = mat[...] - jnp.where(below, update, 0.0)


def spread_kernel(
    mine, rows_out, cols_out, rows, cols, column, corner, mat,
    send_sem, row_sem, column_sem, col_sem, corner_sem,
):
    x, z, core = place(lax.axis_index("row"), lax.axis_index("col"))
    owner = x < 2
    root = x // 2 == z % 2
    other = 1 - core
    side = x + 1 - x % 2 * 2

    def remote(src, dst, arrived, tx, tz, tcore):
        return pltpu.make_async_remote_copy(
            src_ref=src, dst_ref=dst, send_sem=send_sem, recv_sem=arrived,
            device_id=device(tx, tz, tcore), device_id_type=pl.DeviceIdType.MESH,
        )

    def arrive(ref, sem):
        pltpu.make_async_copy(ref, ref, sem).wait()

    def corner_out(act):
        @pl.when(owner & (z == 0))
        def _():
            for dz in range(1, 4):
                act(remote(mine.at[0], corner.at[x, core], corner_sem.at[x, core], x, (z + dz) % 4, core))

    def corner_across(act):
        @pl.when(owner)
        def _():
            for dx in range(1, 4):
                act(
                    remote(
                        corner.at[x, core], corner.at[x, core], corner_sem.at[x, core], (x + dx) % 4, z, core
                    )
                )

    def corner_swap(v, act):
        act(remote(corner.at[v, core], corner.at[v, core], corner_sem.at[v, core], x, z, other))

    def row_out(s, act):
        @pl.when(owner)
        def _():
            act(remote(mine.at[s], rows.at[core, s], row_sem.at[core, s], (x + 2) % 4, z, core))

    def row_swap(s, act):
        act(remote(rows.at[core, s], rows.at[core, s], row_sem.at[core, s], x, z, other))

    def down_column(s, act):
        @pl.when(root)
        def _():
            for dz in range(1, 4):
                act(
                    remote(
                        rows.at[core, s], column.at[z // 2, s], column_sem.at[z // 2, s], x, (z + dz) % 4, core
                    )
                )

    def to_side(n, act):
        h, s = n % 2, n // 2
        act(remote(column.at[h, s], cols.at[h, core, s], col_sem.at[h, core, s], side, z, x % 2))

        @pl.when(core != x % 2)
        def _():
            act(remote(column.at[h, s], cols.at[h, core, s], col_sem.at[h, core, s], x, z, other))

    start = lambda copy: copy.start()
    barrier = pltpu.get_barrier_semaphore()
    greet_neighbours(barrier, x, z, core)
    corner_out(start)

    @pl.when(owner & (z == 0))
    def _():
        pltpu.make_async_copy(mine.at[0], corner.at[x, core], corner_sem.at[x, core]).start()

    def first(s, carry):
        row_out(s, start)

        @pl.when(owner)
        def _():
            pltpu.make_async_copy(mine.at[s], rows.at[core, s], row_sem.at[core, s]).start()

        return carry

    lax.fori_loop(0, 9, first, 0)

    @pl.when(owner)
    def _():
        arrive(corner.at[x, core], corner_sem.at[x, core])

    corner_across(start)

    @pl.when(x != 0)
    def _():
        arrive(corner.at[0, core], corner_sem.at[0, core])

    corner_swap(0, start)

    @pl.when(x != 1)
    def _():
        arrive(corner.at[1, core], corner_sem.at[1, core])

    corner_swap(1, start)

    def second(s, carry):
        arrive(rows.at[core, s], row_sem.at[core, s])
        row_swap(s, start)
        down_column(s, start)

        @pl.when(root)
        def _():
            pltpu.make_async_copy(rows.at[core, s], column.at[z // 2, s], column_sem.at[z // 2, s]).start()

        return carry

    lax.fori_loop(0, 9, second, 0)
    for v in range(2):
        arrive(corner.at[v, other], corner_sem.at[v, other])
    r = lax.broadcasted_iota(jnp.int32, (2 * BLK, 2 * BLK), 0)
    k = lax.broadcasted_iota(jnp.int32, (2 * BLK, 2 * BLK), 1)
    mat[:, pl.ds(2 * BLK, 2 * BLK)] = jnp.where(r == k, 1.0, 0.0)
    for v in range(2):
        for p in range(2):
            mat[pl.ds(v * BLK, BLK), pl.ds(p * BLK, BLK)] = corner[v, p]

    def third(n, carry):
        h, s = n % 2, n // 2
        arrive(column.at[h, s], column_sem.at[h, s])
        to_side(n, start)

        @pl.when(core == x % 2)
        def _():
            pltpu.make_async_copy(column.at[h, s], cols.at[h, core, s], col_sem.at[h, core, s]).start()

        for part in range(2):

            @pl.when(n < 16)
            def _():
                factor_rows(n * 2 + part, mat)

        return carry

    lax.fori_loop(0, 18, third, 0)

    def solve(pair):
        return lax.dot_general(
            pair, mat[:, pl.ds(2 * BLK, 2 * BLK)], (((1,), (1,)), ((), ())),
            precision=HIGH, preferred_element_type=F32,
        )

    def solve_row(s, carry):
        arrive(rows.at[other, s], row_sem.at[other, s])
        rows_out[s] = solve(jnp.concatenate([rows[0, s], rows[1, s]], axis=1))
        return carry

    lax.fori_loop(0, 9, solve_row, 0)

    def solve_col(n, carry):
        h, s = n % 2, n // 2
        for p in range(2):
            arrive(cols.at[h, p, s], col_sem.at[h, p, s])
        hi, lo = split(solve(jnp.concatenate([cols[h, 0, s], cols[h, 1, s]], axis=1)))
        cols_out[n, :, pl.ds(0, 2 * BLK)] = hi
        cols_out[n, :, pl.ds(2 * BLK, 2 * BLK)] = lo
        return carry

    lax.fori_loop(0, 18, solve_col, 0)
    done = lambda copy: copy.wait_send()
    corner_out(done)
    corner_across(done)
    for v in range(2):
        corner_swap(v, done)

    def last(s, carry):
        row_out(s, done)
        row_swap(s, done)
        down_column(s, done)
        to_side(s * 2, done)
        to_side(s * 2 + 1, done)
        return carry

    lax.fori_loop(0, 9, last, 0)


def spread(mine):
    return pl.pallas_call(
        spread_kernel,
        out_shape=(
            jax.ShapeDtypeStruct((9, BLK, 2 * BLK), F32),
            jax.ShapeDtypeStruct((18, BLK, 4 * BLK), BF16),
        ),
        in_specs=[pl.BlockSpec(memory_space=pltpu.VMEM)],
        out_specs=(pl.BlockSpec(memory_space=pltpu.VMEM), pl.BlockSpec(memory_space=pltpu.VMEM)),
        scratch_shapes=[
            pltpu.VMEM((2, 9, BLK, BLK), F32),
            pltpu.VMEM((2, 2, 9, BLK, BLK), F32),
            pltpu.VMEM((2, 9, BLK, BLK), F32),
            pltpu.VMEM((2, 2, BLK, BLK), F32),
            pltpu.VMEM((2 * BLK, 4 * BLK), F32),
            pltpu.SemaphoreType.DMA(()),
            pltpu.SemaphoreType.DMA((2, 9)),
            pltpu.SemaphoreType.DMA((2, 9)),
            pltpu.SemaphoreType.DMA((2, 2, 9)),
            pltpu.SemaphoreType.DMA((2, 2)),
        ],
        compiler_params=pltpu.CompilerParams(
            collective_id=1, has_side_effects=True, vmem_limit_bytes=40 << 20
        ),
        name="spread",
    )(mine)


def final_kernel(tab, code, pos, recv0, recv1, front, rows, cols, out):
    s = pl.program_id(0)
    own_row, own_col = pos[0], pos[1]

    lead = (s == 0) & (own_row < 2)

    @pl.when(lead)
    def _():
        out[...] = jnp.zeros_like(out)

        @pl.when(own_col < 2)
        def _():
            r = lax.broadcasted_iota(jnp.int32, (BLK, BLK), 0) + own_row * BLK
            k = lax.broadcasted_iota(jnp.int32, (BLK, BLK), 1) + own_col * BLK
            mine = jnp.where(own_col == 0, rows[0, :, pl.ds(0, BLK)], rows[0, :, pl.ds(BLK, BLK)])
            out[:, pl.ds(0, BLK)] = jnp.where(r >= k, mine, 0.0)

    @pl.when(jnp.logical_not(lead))
    def _():
        hi, lo = split(rows[0])
        left = jnp.concatenate([hi, lo, hi], axis=1)
        for t in range(18):
            part = pl.ds(t * BLK, BLK)
            right = jnp.concatenate(
                [cols[t, :, pl.ds(0, 256)], cols[t, :, pl.ds(0, 256)], cols[t, :, pl.ds(256, 256)]], axis=1
            )
            val = front[:, part].astype(F32) - lax.dot_general(
                left, right, (((1,), (1,)), ((), ())), preferred_element_type=F32
            )
            for c, recv in enumerate((recv0, recv1)):
                u = code[c, s, t]
                val += jnp.where(u >= 0, recv[0, jnp.maximum(u, 0), t % 2, 0].astype(F32), 0.0)
            out[:, part] = val

        @pl.when(own_col < 2)
        def _():
            out[:, pl.ds(0, BLK)] = jnp.where(own_col == 0, rows[0, :, pl.ds(0, BLK)], rows[0, :, pl.ds(BLK, BLK)])


def final(tab, code, pos, recv, front, rows, cols):
    def recv_spec(c):
        return pl.BlockSpec(
            (1, 8, 2, 1, BLK, BLK), lambda s, tab, code, pos: (tab[c, s], 0, 0, c, 0, 0)
        )

    return pl.pallas_call(
        final_kernel,
        out_shape=jax.ShapeDtypeStruct((9 * BLK, 18 * BLK), F32),
        grid_spec=pltpu.PrefetchScalarGridSpec(
            num_scalar_prefetch=3,
            grid=(9,),
            in_specs=[
                recv_spec(0),
                recv_spec(1),
                pl.BlockSpec((BLK, 18 * BLK), lambda s, *_: (s, 0)),
                pl.BlockSpec((1, BLK, 2 * BLK), lambda s, *_: (s, 0, 0)),
                pl.BlockSpec((18, BLK, 4 * BLK), lambda s, *_: (0, 0, 0)),
            ],
            out_specs=pl.BlockSpec((BLK, 18 * BLK), lambda s, *_: (s, 0)),
        ),
        compiler_params=pltpu.CompilerParams(vmem_limit_bytes=40 << 20),
        name="final",
    )(tab, code, pos, recv, recv, front, rows, cols)


def shards(front_entries, children, child_maps):
    own_row = lax.axis_index("row")
    own_col = lax.axis_index("col")
    pos = jnp.stack([own_row, own_col]).astype(jnp.int32)
    recv = exchange(pack(children, child_maps, pos))
    tab, code = slot_tables(child_maps, own_row, own_col)
    mine = panel(recv, front_entries, tab, code)
    recv = recv.reshape(8, 8, 2, 2, BLK, BLK)
    rows, cols = spread(mine)
    return final(tab, code, pos, recv, front_entries, rows, cols)


def solution(mesh):
    in_specs = (P(("front", "row"), "col"), P("front", "row", "col"), P("front", None))
    out_specs = P(("front", "row"), "col")
    return jax.shard_map(shards, mesh=mesh, in_specs=in_specs, out_specs=out_specs, check_vma=False)
```

time: 472 us -> 207 us (0.44)
  the two profiles are of different devices: /device:TPU:13 before, /device:TPU:80 now
where the time goes in v2:
time: 207 us; the launch traced here: 206 us
  Pallas kernels  191 us (92%)
  local copies, waits for them, and re-layouts  11 us (5%)
  other arithmetic  3.5 us (2%)
    pallas_call x1, Pallas kernels, exchange(): pl.pallas_call(exchange_kernel, out_shape=jax.ShapeDtypeStruct((64, 2, 2,...  97.7 us
    pallas_call x1, Pallas kernels, spread(): pl.pallas_call(spread_kernel, out_shape=(jax.ShapeDtypeStruct((9, BLK, 2...  70.2 us
    pallas_call x1, Pallas kernels, final(): pl.pallas_call(final_kernel, out_shape=jax.ShapeDtypeStruct((9 * BLK, 18...  15.3 us
    unnamed x14, local copies, waits for them, and re-layouts  10.9 us
    pallas_call x1, Pallas kernels, pack(): pl.pallas_call(pack_kernel, out_shape=jax.ShapeDtypeStruct((2, 4, 4, 2, 2...  4.98 us

profile of v2, /device:TPU:80, one launch (start us, length us, event | category | flops | bytes accessed | tf_op | source)
XLA Modules:
  0.0 205.9 jit_solution(10533459949545054391)
XLA Ops:
  0.0 0.1 pad_add_fusion.pos
  0.1 1.0 fusion.1
  1.1 0.1 copy.8
  1.2 0.6 broadcast_maximum_fusion.tab
  1.8 1.1 fusion
  2.9 0.1 copy.10
  3.0 0.7 and_select_fusion.code
  3.7 0.0 copy-start.6
  3.7 0.7 copy-done.6
  4.4 5.0 %pack.1.packed = bf16[2,4,4,2,2,2,128,128]{7,6,5,4,3,2,1,0:T(8,128)(2,1)S(1)} custom-call(s32[2,64]{1,0:T(2,128)S(1)} %copy-done.6, s32[2]{0:T(128)S(1)} %pad_add_fusion.pos, bf16[2,1024,2048]{2,1,0:T(8,128)(2,1)} %children.1), custom_call_target="tpu_custom_call" | custom-call | tf_op jit(solution)/shard_map/pack/pallas_call | solution.py:45
  9.4 0.0 copy-start.1
  9.4 3.4 %copy-done.1 = bf16[2,4,4,2,2,2,128,128]{7,6,5,4,3,2,1,0:T(8,128)(2,1)} copy-done((bf16[2,4,4,2,2,2,128,128]{7,6,5,4,3,2,1,0:T(8,128)(2,1)}, bf16[2,4,4,2,2,2,128,128]{7,6,5,4,3,2,1,0:T(8,128)(2,1)S(1)}, u32[]{:S(2)}) %copy-start.1) | copy-done | bytes 8388632
  12.8 97.7 %exchange.1.recv = bf16[64,2,2,128,128]{4,3,2,1,0:T(8,128)(2,1)S(1)} custom-call(bf16[2,4,4,2,2,2,128,128]{7,6,5,4,3,2,1,0:T(8,128)(2,1)} %copy-done.1), custom_call_target="tpu_custom_call" | custom-call | tf_op jit(solution)/shard_map/exchange/pallas_call | solution.py:240
  110.5 0.0 copy-start
  110.5 3.2 %copy-done = bf16[64,2,2,128,128]{4,3,2,1,0:T(8,128)(2,1)} copy-done((bf16[64,2,2,128,128]{4,3,2,1,0:T(8,128)(2,1)}, bf16[64,2,2,128,128]{4,3,2,1,0:T(8,128)(2,1)S(1)}, u32[]{:S(2)}) %copy-start) | copy-done | bytes 8388632
  113.7 3.1 %panel.1.mine = f32[9,128,128]{2,1,0:T(8,128)} custom-call(s32[2,9]{1,0:T(2,128)} %broadcast_maximum_fusion.tab, s32[2,9,18]{2,1,0:T(8,128)} %and_select_fusion.code, bf16[64,2,2,128,128]{4,3,2,1,0:T(8,128)(2,1)} %copy-done, bf16[1152,2304]{1,0:T(8,128)(2,1)} %front.3), custom_call_target="tpu_custom_call" | custom-call | tf_op jit(solution)/shard_map/panel/pallas_call | solution.py:286
  116.8 0.0 copy-start.3
  116.9 1.1 copy-done.3
  117.9 70.2 %spread.1 = (f32[9,128,256]{2,1,0:T(8,128)S(1)}, bf16[18,128,512]{2,1,0:T(8,128)(2,1)S(1)}) custom-call(f32[9,128,128]{2,1,0:T(8,128)S(1)} %copy-done.3), custom_call_target="tpu_custom_call" | custom-call | tf_op jit(solution)/shard_map/spread/pallas_call | solution.py:516
  188.1 0.0 copy-done.4
  188.1 0.0 copy-done.5
  188.1 0.0 copy-start.2
  188.1 2.5 %copy-done.2 = bf16[1152,2304]{1,0:T(8,128)(2,1)S(1)} copy-done((bf16[1152,2304]{1,0:T(8,128)(2,1)S(1)}, bf16[1152,2304]{1,0:T(8,128)(2,1)}, u32[]{:S(2)}) %copy-start.2) | copy-done | bytes 5308440
  190.6 15.3 %final.1 = f32[1152,2304]{1,0:T(8,128)} custom-call(s32[2,9]{1,0:T(2,128)S(1)} %copy-done.5, s32[2,9,18]{2,1,0:T(8,128)S(1)} %copy-done.4, s32[2]{0:T(128)S(1)} %pad_add_fusion.pos, bf16[8,8,2,2,128,128]{5,4,3,2,1,0:T(8,128)(2,1)} %bitcast.3, bf16[8,8,2,2,128,128]{5,4,3,2,1,0:T(8,128)(2,1)} %bitcast.4, bf16[1152,2304]{1,0:T(8,128)(2,1)S(1)} %copy-done.2, ...), custom_call_target="tpu_custom_call" | custom-call | tf_op jit(solution)/shard_map/final/pallas_call | solution.py:588
  (8 shorter events, 0.0 us)
Async XLA Ops:
  3.7 0.7 copy-start.6
  9.4 3.4 %copy-start.1 = (bf16[2,4,4,2,2,2,128,128]{7,6,5,4,3,2,1,0:T(8,128)(2,1)}, bf16[2,4,4,2,2,2,128,128]{7,6,5,4,3,2,1,0:T(8,128)(2,1)S(1)}, u32[]{:S(2)}) copy-start(bf16[2,4,4,2,2,2,128,128]{7,6,5,4,3,2,1,0:T(8,128)(2,1)S(1)} %pack.1.packed) | copy-start | bytes 25165828
  110.5 3.2 %copy-start = (bf16[64,2,2,128,128]{4,3,2,1,0:T(8,128)(2,1)}, bf16[64,2,2,128,128]{4,3,2,1,0:T(8,128)(2,1)S(1)}, u32[]{:S(2)}) copy-start(bf16[64,2,2,128,128]{4,3,2,1,0:T(8,128)(2,1)S(1)} %exchange.1.recv) | copy-start | bytes 25165828
  113.7 74.3 %copy-start.4 = (s32[2,9,18]{2,1,0:T(8,128)S(1)}, s32[2,9,18]{2,1,0:T(8,128)}, u32[]{:S(2)}) copy-start(s32[2,9,18]{2,1,0:T(8,128)} %and_select_fusion.code) | copy-start | bytes 3892
  113.7 74.4 %copy-start.5 = (s32[2,9]{1,0:T(2,128)S(1)}, s32[2,9]{1,0:T(2,128)}, u32[]{:S(2)}) copy-start(s32[2,9]{1,0:T(2,128)} %broadcast_maximum_fusion.tab) | copy-start | bytes 220
  116.8 1.1 copy-start.3
  188.1 2.5 %copy-start.2 = (bf16[1152,2304]{1,0:T(8,128)(2,1)S(1)}, bf16[1152,2304]{1,0:T(8,128)(2,1)}, u32[]{:S(2)}) copy-start(bf16[1152,2304]{1,0:T(8,128)(2,1)} %front.3) | copy-start | bytes 15925252

commit v3 on v2

v3 whole, which is shorter than its diff:
```python
import jax
import jax.numpy as jnp
from jax import lax
from jax.experimental import pallas as pl
from jax.experimental.pallas import tpu as pltpu
from jax.sharding import PartitionSpec as P

BLK = 128
F32 = jnp.float32
BF16 = jnp.bfloat16
HIGH = lax.Precision.HIGHEST


def pack_kernel(maps, children, out, rows_of, cols_of, buf, packed, row_of, col_of, in_sem, out_sem):
    own_row, own_col = lax.axis_index("row"), lax.axis_index("col")
    for c in range(2):
        for k in range(8):
            row_of[c, maps[c, k * 8 + own_row] % 8] = k
        for k in range(16):
            col_of[c, (k % 2) * 8 + maps[c, k * 4 + own_col] % 8] = k
    for d in range(8):
        for c in range(2):
            pltpu.make_async_copy(
                children.at[c, pl.ds(row_of[c, d] * BLK, BLK), :], buf.at[d, c], in_sem.at[d]
            ).start()
    for c in range(2):
        for s in range(9):
            rows_of[c, s] = -1
        for t in range(18):
            cols_of[c, t] = -1

        def look(k, carry):
            v = maps[c, k]

            @pl.when(v % 8 == own_row)
            def _():
                rows_of[c, v // 8] = k % 8

            @pl.when(v % 4 == own_col)
            def _():
                cols_of[c, v // 4] = k % 4 * 2 + k % 8 // 4

            return carry

        lax.fori_loop(0, 64, look, 0, unroll=8)

    def one_row(d, carry):
        for c in range(2):
            pltpu.make_async_copy(children.at[0, pl.ds(0, BLK), :], buf.at[d, c], in_sem.at[d]).wait()
        for c in range(2):
            for half in range(2):
                for delta in range(8):
                    start = pl.multiple_of(col_of[c, half * 8 + delta] * BLK, BLK)
                    packed[half, d % 4, delta % 4, d // 4, delta // 4, c] = buf[d, c, :, pl.ds(start, BLK)]
        pltpu.make_async_copy(
            packed.at[:, d % 4, :, d // 4], out.at[:, d % 4, :, d // 4], out_sem.at[0]
        ).start()
        return carry

    lax.fori_loop(0, 8, one_row, 0)
    pltpu.make_async_copy(packed, out, out_sem.at[0]).wait()


def pack(children, child_maps):
    return pl.pallas_call(
        pack_kernel,
        out_shape=(
            jax.ShapeDtypeStruct((2, 4, 4, 2, 2, 2, BLK, BLK), BF16),
            jax.ShapeDtypeStruct((2, 9), jnp.int32),
            jax.ShapeDtypeStruct((2, 18), jnp.int32),
        ),
        in_specs=[pl.BlockSpec(memory_space=pltpu.SMEM), pl.BlockSpec(memory_space=pl.ANY)],
        out_specs=(
            pl.BlockSpec(memory_space=pl.ANY),
            pl.BlockSpec(memory_space=pltpu.SMEM),
            pl.BlockSpec(memory_space=pltpu.SMEM),
        ),
        scratch_shapes=[
            pltpu.VMEM((8, 2, BLK, 16 * BLK), BF16),
            pltpu.VMEM((2, 4, 4, 2, 2, 2, BLK, BLK), BF16),
            pltpu.SMEM((2, 8), jnp.int32),
            pltpu.SMEM((2, 16), jnp.int32),
            pltpu.SemaphoreType.DMA((8,)),
            pltpu.SemaphoreType.DMA((1,)),
        ],
        compiler_params=pltpu.CompilerParams(vmem_limit_bytes=60 << 20),
        name="pack",
    )(child_maps, children)


def identity():
    r = lax.broadcasted_iota(jnp.int32, (BLK, BLK), 0)
    k = lax.broadcasted_iota(jnp.int32, (BLK, BLK), 1)
    return jnp.where(r == k, 1.0, 0.0).astype(BF16)


def place(row, col):
    return col // 2 * 2 + row % 2, row // 2, col % 2


def device(x, z, core):
    return {"row": z * 2 + x % 2, "col": x // 2 * 2 + core}


def ring(t):
    t = (t + 4) % 4
    return t - 2 * (t // 3)


def apart(x, z, tx, tz):
    return ring(tx - x) + ring(tz - z)


def wants(x, z, core, tx, tz, half):
    a, b = z * 2 + x % 2, x // 2 * 2 + core
    alpha = b + 4 * half
    ox, oz, _ = place(alpha, a % 4)
    here, there = apart(x, z, tx, tz), apart(ox, oz, tx, tz)
    return here <= there, here < there


def unit(packed, x, z, core, tx, tz, tcore, half, kind, h):
    a, b = z * 2 + x % 2, x // 2 * 2 + core
    alpha = b + 4 * half
    d, e = tz * 2 + tx % 2, tx // 2 * 2 + tcore
    if kind == 0:
        return packed.at[half, d % 4, e, d // 4, h], a * 8 + b * 2 + half
    return packed.at[half, e, d % 4, h, d // 4], alpha * 8 + a % 4 * 2 + a // 4


def far_step(n):
    k = n % 3
    return 2 - k + 3 * (k // 2), 1 + n // 6, n // 3 % 2


def near_step(n):
    dx = (1 - n // 6) * (1 - n // 12) * (n // 2 + 1)
    dz = n // 6 * (1 - n // 12) * ((n - 6) // 2 + 1)
    return dx, dz, n % 2 * (1 - n // 12) + n // 12


def greet_neighbours(barrier, x, z, core):
    def greet(n, carry):
        dx, dz, dc = near_step(n)
        pl.semaphore_signal(
            barrier, inc=1, device_id=device((x + dx) % 4, (z + dz) % 4, (core + dc) % 2),
            device_id_type=pl.DeviceIdType.MESH,
        )
        return carry

    lax.fori_loop(0, 13, greet, 0)
    pl.semaphore_wait(barrier, 13)


def split(x):
    hi = x.astype(BF16)
    lo = (x - hi.astype(F32)).astype(BF16)
    return hi, lo


def pieces(x):
    a = x.astype(BF16).astype(F32)
    b = (x - a).astype(BF16).astype(F32)
    return a, b, x - a - b


def factor_rows(r, mat, base):
    span = pl.ds(base, 3 * BLK)
    lane = lax.broadcasted_iota(jnp.int32, (8, 2 * BLK - base), 1) + base
    wide = lax.broadcasted_iota(jnp.int32, (8, 3 * BLK), 1) + base
    sub = lax.broadcasted_iota(jnp.int32, (8, 1), 0)
    rows = pl.ds(pl.multiple_of(r * 8, 8), 8)
    w = mat[rows, span]
    head = w[:, : 2 * BLK - base]
    col = [jnp.sum(jnp.where(lane == r * 8 + j, head, 0.0), axis=1, keepdims=True) for j in range(8)]
    for j in range(8):
        pivot = col[j][j : j + 1]
        inv = lax.rsqrt(pivot)
        inv = inv * (1.5 - 0.5 * pivot * inv * inv)
        mult = jnp.where(sub > j, col[j] * inv, 0.0)
        for k in range(j + 1, 8):
            col[k] = col[k] - mult * (col[k][j : j + 1] * inv)
        top = w[j : j + 1] * inv
        w = jnp.where(sub == j, top, w - mult * top)
    w = jnp.where(wide < r * 8 + sub, 0.0, w)
    mat[rows, span] = w
    a, b, c = pieces(w)
    u = [part[:, : 2 * BLK - base] for part in (a, a, b, a, c, b)]
    left = jnp.concatenate(u, axis=0).astype(BF16)
    right = jnp.concatenate([a, b, a, c, a, b], axis=0).astype(BF16)
    update = lax.dot_general(left, right, (((0,), (0,)), ((), ())), preferred_element_type=F32)
    below = lax.broadcasted_iota(jnp.int32, (2 * BLK - base, 1), 0) + base >= (r + 1) * 8
    rest = pl.ds(base, 2 * BLK - base)
    mat[rest, span] = mat[rest, span] - jnp.where(below, update, 0.0)


def front_kernel(
    row_tab, col_tab, packed, front, out_a, out_b, rows_out, cols_out,
    recv_a, recv_b, hold, mine, rows, cols, column, corner, mat, rows_sol, cols_sol, inv,
    send_sem, recv_sem, hold_sem, row_sem, column_sem, col_sem, corner_sem, out_sem,
):
    x, z, core = place(lax.axis_index("row"), lax.axis_index("col"))
    owner = x < 2
    root = x // 2 == z % 2
    other = 1 - core
    side = x + 1 - x % 2 * 2
    recv = (recv_a, recv_b)
    start = lambda copy: copy.start()
    done = lambda copy: copy.wait_send()

    def remote(src, dst, arrived, tx, tz, tcore):
        return pltpu.make_async_remote_copy(
            src_ref=src, dst_ref=dst, send_sem=send_sem, recv_sem=arrived,
            device_id=device(tx, tz, tcore), device_id_type=pl.DeviceIdType.MESH,
        )

    def arrive(ref, sem):
        pltpu.make_async_copy(ref, ref, sem).wait()

    def loop(lo, hi, body):
        def step(n, carry):
            body(n)
            return carry

        lax.fori_loop(lo, hi, step, 0)

    def each(sx, sz, tx, tz, fn):
        for half in range(2):
            for kind, wanted in enumerate(wants(sx, sz, core, tx, tz, half)):
                for h in range(2):

                    @pl.when(wanted)
                    def _():
                        fn(half, kind, h)

    def far(n, act):
        dz, dx, dc = far_step(n)
        tx, tz, tcore = (x + dx) % 4, (z + dz) % 4, (core + dc) % 2

        def one(half, kind, h):
            src, _ = unit(packed, x, z, core, tx, tz, tcore, half, kind, h)
            slot = n * 4 + half * 2 + kind
            act(remote(src, hold.at[slot, h], hold_sem.at[slot, h], x, tz, core))

        each(x, z, tx, tz, one)

    def near(n, act):
        dx, dz, dc = near_step(n)
        tx, tz, tcore = (x + dx) % 4, (z + dz) % 4, (core + dc) % 2

        def one(half, kind, h):
            src, dst = unit(packed, x, z, core, tx, tz, tcore, half, kind, h)
            act(remote(src, recv[h].at[dst], recv_sem.at[dst, h], tx, tz, tcore))

        each(x, z, tx, tz, one)

    def own():
        def one(half, kind, h):
            src, dst = unit(packed, x, z, core, x, z, core, half, kind, h)
            pltpu.make_async_copy(src, recv[h].at[dst], recv_sem.at[dst, h]).start()

        each(x, z, x, z, one)

    def pass_on(n, act, wait):
        dz, dx, dc = far_step(n)
        sz = (z - dz + 4) % 4
        tx, tcore = (x + dx) % 4, (core + dc) % 2

        def one(half, kind, h):
            _, dst = unit(packed, x, sz, core, tx, z, tcore, half, kind, h)
            slot = n * 4 + half * 2 + kind
            if wait:
                arrive(hold.at[slot, h], hold_sem.at[slot, h])
            act(remote(hold.at[slot, h], recv[h].at[dst], recv_sem.at[dst, h], tx, z, tcore))

        each(x, sz, tx, z, one)

    def settle(slot, h):
        arrive(recv[h].at[slot], recv_sem.at[slot, h])
        row, u = slot // 8, slot % 8
        alpha = u // 2 + u % 2 * 4
        nx, nz, _ = place(row, alpha % 4)
        ox, oz, _ = place(alpha, row % 4)

        @pl.when(apart(ox, oz, x, z) < apart(nx, nz, x, z))
        def _():
            for c in range(2):
                recv[h][slot, c] = lax.dot_general(
                    identity(), recv[h][slot, c], (((1,), (1,)), ((), ())), preferred_element_type=F32
                ).astype(BF16)

    def corner_out(act):
        @pl.when(owner & (z == 0))
        def _():
            for dz in range(1, 4):
                act(remote(mine.at[0], corner.at[x, core], corner_sem.at[x, core], x, (z + dz) % 4, core))

    def corner_across(act):
        @pl.when(owner)
        def _():
            for dx in range(1, 4):
                act(
                    remote(
                        corner.at[x, core], corner.at[x, core], corner_sem.at[x, core], (x + dx) % 4, z, core
                    )
                )

    def corner_swap(v, act):
        act(remote(corner.at[v, core], corner.at[v, core], corner_sem.at[v, core], x, z, other))

    def row_out(s, act):
        @pl.when(owner)
        def _():
            act(remote(mine.at[s], rows.at[core, s], row_sem.at[core, s], (x + 2) % 4, z, core))

    def row_swap(s, act):
        act(remote(rows.at[core, s], rows.at[core, s], row_sem.at[core, s], x, z, other))

    def down_column(s, act):
        @pl.when(root)
        def _():
            for dz in range(1, 4):
                act(
                    remote(
                        rows.at[core, s], column.at[z // 2, s], column_sem.at[z // 2, s], x, (z + dz) % 4, core
                    )
                )

    def to_side(n, act):
        h, s = n % 2, n // 2
        act(remote(column.at[h, s], cols.at[h, core, s], col_sem.at[h, core, s], side, z, x % 2))

        @pl.when(core != x % 2)
        def _():
            act(remote(column.at[h, s], cols.at[h, core, s], col_sem.at[h, core, s], x, z, other))

    barrier = pltpu.get_barrier_semaphore()
    greet_neighbours(barrier, x, z, core)

    loop(0, 6, lambda n: near(n, start))
    loop(0, 18, lambda n: far(n, start))
    loop(6, 13, lambda n: near(n, start))
    own()
    loop(0, 18, lambda n: pass_on(n, start, True))
    @pl.when(owner)
    def _():
        loop(0, 64, lambda slot: settle(slot, 0))
        for s in range(9):
            total = front[pl.ds(s * BLK, BLK), :].astype(F32)
            for c in range(2):
                row, u = row_tab[c, s], col_tab[c, 0]
                blk = recv_a[jnp.maximum(row, 0) * 8 + jnp.maximum(u, 0), c].astype(F32)
                total += jnp.where((row >= 0) & (u >= 0), blk, 0.0)
            mine[s] = total

    corner_out(start)

    @pl.when(owner & (z == 0))
    def _():
        pltpu.make_async_copy(mine.at[0], corner.at[x, core], corner_sem.at[x, core]).start()

    def first(s):
        row_out(s, start)

        @pl.when(owner)
        def _():
            pltpu.make_async_copy(mine.at[s], rows.at[core, s], row_sem.at[core, s]).start()

    loop(0, 9, first)

    def second(s):
        arrive(rows.at[core, s], row_sem.at[core, s])
        row_swap(s, start)
        down_column(s, start)

        @pl.when(root)
        def _():
            pltpu.make_async_copy(rows.at[core, s], column.at[z // 2, s], column_sem.at[z // 2, s]).start()

    loop(0, 9, second)

    @pl.when(owner)
    def _():
        arrive(corner.at[x, core], corner_sem.at[x, core])

    corner_across(start)

    @pl.when(x != 0)
    def _():
        arrive(corner.at[0, core], corner_sem.at[0, core])

    corner_swap(0, start)

    @pl.when(x != 1)
    def _():
        arrive(corner.at[1, core], corner_sem.at[1, core])

    corner_swap(1, start)
    for v in range(2):
        arrive(corner.at[v, other], corner_sem.at[v, other])
    r = lax.broadcasted_iota(jnp.int32, (2 * BLK, 2 * BLK), 0)
    k = lax.broadcasted_iota(jnp.int32, (2 * BLK, 2 * BLK), 1)
    mat[:, pl.ds(2 * BLK, 2 * BLK)] = jnp.where(r == k, 1.0, 0.0)
    for v in range(2):
        for p in range(2):
            mat[pl.ds(v * BLK, BLK), pl.ds(p * BLK, BLK)] = corner[v, p]

    def fourth(n):
        h, s = n % 2, n // 2
        arrive(column.at[h, s], column_sem.at[h, s])
        to_side(n, start)

        @pl.when(core == x % 2)
        def _():
            pltpu.make_async_copy(column.at[h, s], cols.at[h, core, s], col_sem.at[h, core, s]).start()

        for g in range(2):

            @pl.when((n >= g * 8) & (n < g * 8 + 8))
            def _():
                factor_rows(n * 2, mat, g * BLK)
                factor_rows(n * 2 + 1, mat, g * BLK)

    loop(0, 18, fourth)

    inv_hi, inv_lo = split(mat[:, pl.ds(2 * BLK, 2 * BLK)])
    inv[:, pl.ds(0, 2 * BLK)] = inv_hi
    inv[:, pl.ds(2 * BLK, 2 * BLK)] = inv_hi
    inv[:, pl.ds(4 * BLK, 2 * BLK)] = inv_lo

    def solve(left, right):
        pair = jnp.concatenate([left.reshape(3 * BLK, BLK), right.reshape(3 * BLK, BLK)], axis=1)
        hi, lo = split(pair)
        return lax.dot_general(
            jnp.concatenate([hi, lo, hi], axis=1), inv[...], (((1,), (1,)), ((), ())), preferred_element_type=F32
        )

    def solve_row(i):
        for j in range(3):
            arrive(rows.at[other, i * 3 + j], row_sem.at[other, i * 3 + j])
        three = pl.ds(i * 3, 3)
        rows_sol[three] = solve(rows[0, three], rows[1, three]).reshape(3, BLK, 2 * BLK)

    loop(0, 3, solve_row)

    def late(slot):
        settle(slot, 1)

        @pl.when(jnp.logical_not(owner))
        def _():
            settle(slot, 0)

    loop(0, 64, late)
    outs = [
        pltpu.make_async_copy(recv_a, out_a, out_sem.at[0]),
        pltpu.make_async_copy(recv_b, out_b, out_sem.at[1]),
        pltpu.make_async_copy(rows_sol, rows_out, out_sem.at[2]),
    ]
    for copy in outs:
        copy.start()

    def solve_col(n):
        h, i = n % 2, n // 2
        for p in range(2):
            for j in range(3):
                arrive(cols.at[h, p, i * 3 + j], col_sem.at[h, p, i * 3 + j])
        three = pl.ds(i * 3, 3)
        hi, lo = split(solve(cols[h, 0, three], cols[h, 1, three]).reshape(3, BLK, 2 * BLK))
        cols_sol[h, three, :, pl.ds(0, 2 * BLK)] = hi
        cols_sol[h, three, :, pl.ds(2 * BLK, 2 * BLK)] = lo

    loop(0, 6, solve_col)
    last = pltpu.make_async_copy(cols_sol, cols_out, out_sem.at[3])
    last.start()

    def finish(n):
        far(n, done)
        pass_on(n, done, False)

        @pl.when(n < 13)
        def _():
            near(n, done)

        to_side(n, done)

        @pl.when(n < 9)
        def _():
            row_out(n, done)
            row_swap(n, done)
            down_column(n, done)

    loop(0, 18, finish)
    corner_out(done)
    corner_across(done)
    for v in range(2):
        corner_swap(v, done)
    for copy in outs:
        copy.wait()
    last.wait()


def front_stage(row_tab, col_tab, packed, front):
    anywhere = pl.BlockSpec(memory_space=pl.ANY)
    return pl.pallas_call(
        front_kernel,
        grid=(1,),
        out_shape=(
            jax.ShapeDtypeStruct((64, 2, BLK, BLK), BF16),
            jax.ShapeDtypeStruct((64, 2, BLK, BLK), BF16),
            jax.ShapeDtypeStruct((9, BLK, 2 * BLK), F32),
            jax.ShapeDtypeStruct((2, 9, BLK, 4 * BLK), BF16),
        ),
        in_specs=[
            pl.BlockSpec(memory_space=pltpu.SMEM),
            pl.BlockSpec(memory_space=pltpu.SMEM),
            anywhere,
            pl.BlockSpec((9 * BLK, BLK), lambda i: (0, 0)),
        ],
        out_specs=(anywhere, anywhere, anywhere, anywhere),
        scratch_shapes=[
            pltpu.VMEM((64, 2, BLK, BLK), BF16),
            pltpu.VMEM((64, 2, BLK, BLK), BF16),
            pltpu.VMEM((72, 2, 2, BLK, BLK), BF16),
            pltpu.VMEM((9, BLK, BLK), F32),
            pltpu.VMEM((2, 9, BLK, BLK), F32),
            pltpu.VMEM((2, 2, 9, BLK, BLK), F32),
            pltpu.VMEM((2, 9, BLK, BLK), F32),
            pltpu.VMEM((2, 2, BLK, BLK), F32),
            pltpu.VMEM((2 * BLK, 4 * BLK), F32),
            pltpu.VMEM((9, BLK, 2 * BLK), F32),
            pltpu.VMEM((2, 9, BLK, 4 * BLK), BF16),
            pltpu.VMEM((2 * BLK, 6 * BLK), BF16),
            pltpu.SemaphoreType.DMA(()),
            pltpu.SemaphoreType.DMA((64, 2)),
            pltpu.SemaphoreType.DMA((72, 2)),
            pltpu.SemaphoreType.DMA((2, 9)),
            pltpu.SemaphoreType.DMA((2, 9)),
            pltpu.SemaphoreType.DMA((2, 2, 9)),
            pltpu.SemaphoreType.DMA((2, 2)),
            pltpu.SemaphoreType.DMA((4,)),
        ],
        compiler_params=pltpu.CompilerParams(
            collective_id=0, has_side_effects=True, vmem_limit_bytes=62 << 20
        ),
        name="front_stage",
    )(row_tab, col_tab, packed, front)


def final_kernel(row_tab, col_tab, *refs):
    recv = [refs[4 * j : 4 * j + 4] for j in range(3)]
    front, rows, cols, out = refs[12:]
    step = pl.program_id(0)
    own_row, own_col = lax.axis_index("row"), lax.axis_index("col")
    hi, lo = split(rows[...].reshape(3 * BLK, 2 * BLK))
    left = jnp.concatenate([hi, lo, hi], axis=1)
    for t in range(18):
        part = pl.ds(t * BLK, BLK)
        right = jnp.concatenate([cols[t % 2, t // 2, :, pl.ds(k, 256)] for k in (0, 0, 256)], axis=1)
        val = front[:, part].astype(F32) - lax.dot_general(
            left, right, (((1,), (1,)), ((), ())), preferred_element_type=F32
        )
        for j in range(3):
            here = val[j * BLK : (j + 1) * BLK]
            for c in range(2):
                u = col_tab[c, t]
                blk = recv[j][c * 2 + t % 2][0, jnp.maximum(u, 0), 0].astype(F32)
                here += jnp.where((u >= 0) & (row_tab[c, step * 3 + j] >= 0), blk, 0.0)
            out[pl.ds(j * BLK, BLK), part] = here

    @pl.when(own_col < 2)
    def _():
        for j in range(3):
            out[pl.ds(j * BLK, BLK), pl.ds(0, BLK)] = jnp.where(
                own_col == 0, rows[j, :, pl.ds(0, BLK)], rows[j, :, pl.ds(BLK, BLK)]
            )

    @pl.when((step == 0) & (own_row < 2))
    def _():
        out[pl.ds(0, BLK), :] = jnp.zeros((BLK, 18 * BLK), F32)

        @pl.when(own_col < 2)
        def _():
            r = lax.broadcasted_iota(jnp.int32, (BLK, BLK), 0) + own_row * BLK
            k = lax.broadcasted_iota(jnp.int32, (BLK, BLK), 1) + own_col * BLK
            mine = jnp.where(own_col == 0, rows[0, :, pl.ds(0, BLK)], rows[0, :, pl.ds(BLK, BLK)])
            out[pl.ds(0, BLK), pl.ds(0, BLK)] = jnp.where(r >= k, mine, 0.0)


def final(row_tab, col_tab, recv_a, recv_b, front, rows, cols):
    def recv_spec(j, c):
        return pl.BlockSpec(
            (1, 8, 1, BLK, BLK),
            lambda step, row_tab, col_tab: (jnp.maximum(row_tab[c, step * 3 + j], 0), 0, c, 0, 0),
        )

    return pl.pallas_call(
        final_kernel,
        out_shape=jax.ShapeDtypeStruct((9 * BLK, 18 * BLK), F32),
        grid_spec=pltpu.PrefetchScalarGridSpec(
            num_scalar_prefetch=2,
            grid=(3,),
            in_specs=[recv_spec(j, c) for j in range(3) for c in range(2) for _ in range(2)]
            + [
                pl.BlockSpec((3 * BLK, 18 * BLK), lambda s, *_: (s, 0)),
                pl.BlockSpec((3, BLK, 2 * BLK), lambda s, *_: (s, 0, 0)),
                pl.BlockSpec((2, 9, BLK, 4 * BLK), lambda s, *_: (0, 0, 0, 0)),
            ],
            out_specs=pl.BlockSpec((3 * BLK, 18 * BLK), lambda s, *_: (s, 0)),
        ),
        compiler_params=pltpu.CompilerParams(vmem_limit_bytes=60 << 20),
        name="final",
    )(row_tab, col_tab, *([recv_a, recv_b] * 6), front, rows, cols)


def shards(front_entries, children, child_maps):
    packed, row_tab, col_tab = pack(children, child_maps)
    recv_a, recv_b, rows, cols = front_stage(row_tab, col_tab, packed, front_entries)
    recv_a, recv_b = (part.reshape(8, 8, 2, BLK, BLK) for part in (recv_a, recv_b))
    return final(row_tab, col_tab, recv_a, recv_b, front_entries, rows, cols)


def solution(mesh):
    in_specs = (P(("front", "row"), "col"), P("front", "row", "col"), P("front", None))
    out_specs = P(("front", "row"), "col")
    return jax.shard_map(shards, mesh=mesh, in_specs=in_specs, out_specs=out_specs, check_vma=False)
```

time: 207 us -> 163 us (0.79)
  the two profiles are of different devices: /device:TPU:80 before, /device:TPU:13 now
where the time goes in v3:
time: 163 us; the launch traced here: 161 us
  Pallas kernels  161 us (99%)
    pallas_call x1, Pallas kernels, front_stage(): pl.pallas_call(front_kernel, grid=(1,), out_shape=(jax.ShapeDtypeStruct((...  137 us
    pallas_call x1, Pallas kernels, final(): pl.pallas_call(final_kernel, out_shape=jax.ShapeDtypeStruct((9 * BLK, 18...  15.7 us
    pallas_call x1, Pallas kernels, pack(): pl.pallas_call(pack_kernel, out_shape=(jax.ShapeDtypeStruct((2, 4, 4, 2,...  8.03 us

profile of v3, /device:TPU:13, one launch (start us, length us, event | category | flops | bytes accessed | tf_op | source)
XLA Modules:
  0.0 161.0 jit_solution(7810432210579045122)
XLA Ops:
  0.0 8.0 %pack.1 = (bf16[2,4,4,2,2,2,128,128]{7,6,5,4,3,2,1,0:T(8,128)(2,1)}, s32[2,9]{1,0:T(2,128)}, s32[2,18]{1,0:T(2,128)}) custom-call(s32[2,64]{1,0:T(2,128)} %maps.1, bf16[2,1024,2048]{2,1,0:T(8,128)(2,1)} %children.1), custom_call_target="tpu_custom_call" | custom-call | tf_op jit(solution)/shard_map/pack/pallas_call | solution.py:65
  8.0 137.2 %front_stage.1 = (bf16[64,2,128,128]{3,2,1,0:T(8,128)(2,1)}, bf16[64,2,128,128]{3,2,1,0:T(8,128)(2,1)}, f32[9,128,256]{2,1,0:T(8,128)}, bf16[2,9,128,512]{3,2,1,0:T(8,128)(2,1)}) custom-call(s32[2,9]{1,0:T(2,128)} %get-tuple-element.12.row_tab, s32[2,18]{1,0:T(2,128)} %get-tuple-element.13.col_tab, ...), custom_call_target="tpu_custom_call" | custom-call | tf_op jit(solution)/shard_map/front_stage/pallas_call | solution.py:504
  145.3 15.7 %final.1 = f32[1152,2304]{1,0:T(8,128)} custom-call(s32[2,9]{1,0:T(2,128)} %get-tuple-element.12.row_tab, s32[2,18]{1,0:T(2,128)} %get-tuple-element.13.col_tab, bf16[8,8,2,128,128]{4,3,2,1,0:T(8,128)(2,1)} %bitcast.2, bf16[8,8,2,128,128]{4,3,2,1,0:T(8,128)(2,1)} %bitcast.8, bf16[8,8,2,128,128]{4,3,2,1,0:T(8,128)(2,1)} %bitcast.3, ...), custom_call_target="tpu_custom_call" | custom-call | tf_op jit(solution)/shard_map/final/pallas_call | solution.py:596

commit v4 on v3

--- a/solution.py
+++ b/solution.py
@@ -15,9 +15,9 @@
     own_row, own_col = lax.axis_index("row"), lax.axis_index("col")
     for c in range(2):
         for k in range(8):
-            row_of[c, maps[c, k * 8 + own_row] % 8] = k
+            row_of[c, maps[c, k * 8 + own_row] & 7] = k
         for k in range(16):
-            col_of[c, (k % 2) * 8 + maps[c, k * 4 + own_col] % 8] = k
+            col_of[c, (k % 2) * 8 + (maps[c, k * 4 + own_col] & 7)] = k
     for d in range(8):
         for c in range(2):
             pltpu.make_async_copy(
@@ -29,20 +29,16 @@
         for t in range(18):
             cols_of[c, t] = -1
 
-        def look(k, carry):
+        for k in range(64):
             v = maps[c, k]
 
-            @pl.when(v % 8 == own_row)
+            @pl.when((v & 7) == own_row)
             def _():
-                rows_of[c, v // 8] = k % 8
-
-            @pl.when(v % 4 == own_col)
+                rows_of[c, v >> 3] = k % 8
+
+            @pl.when((v & 3) == own_col)
             def _():
-                cols_of[c, v // 4] = k % 4 * 2 + k % 8 // 4
-
-            return carry
-
-        lax.fori_loop(0, 64, look, 0, unroll=8)
+                cols_of[c, v >> 2] = k % 4 * 2 + k % 8 // 4
 
     def one_row(d, carry):
         for c in range(2):
@@ -275,8 +271,9 @@
 
         each(x, sz, tx, z, one)
 
-    def settle(slot, h):
-        arrive(recv[h].at[slot], recv_sem.at[slot, h])
+    def settle(slot, halves):
+        for h in halves:
+            arrive(recv[h].at[slot], recv_sem.at[slot, h])
         row, u = slot // 8, slot % 8
         alpha = u // 2 + u % 2 * 4
         nx, nz, _ = place(row, alpha % 4)
@@ -284,10 +281,16 @@
 
         @pl.when(apart(ox, oz, x, z) < apart(nx, nz, x, z))
         def _():
-            for c in range(2):
-                recv[h][slot, c] = lax.dot_general(
-                    identity(), recv[h][slot, c], (((1,), (1,)), ((), ())), preferred_element_type=F32
+            turned = [
+                lax.dot_general(
+                    identity(), recv[h][slot].reshape(2 * BLK, BLK), (((1,), (1,)), ((), ())),
+                    preferred_element_type=F32,
                 ).astype(BF16)
+                for h in halves
+            ]
+            for h, both in zip(halves, turned):
+                for c in range(2):
+                    recv[h][slot, c] = both[:, c * BLK : (c + 1) * BLK]
 
     def corner_out(act):
         @pl.when(owner & (z == 0))
@@ -344,7 +347,7 @@
     loop(0, 18, lambda n: pass_on(n, start, True))
     @pl.when(owner)
     def _():
-        loop(0, 64, lambda slot: settle(slot, 0))
+        loop(0, 64, lambda slot: settle(slot, (0,)))
         for s in range(9):
             total = front[pl.ds(s * BLK, BLK), :].astype(F32)
             for c in range(2):
@@ -377,7 +380,22 @@
         def _():
             pltpu.make_async_copy(rows.at[core, s], column.at[z // 2, s], column_sem.at[z // 2, s]).start()
 
+    @pl.when(jnp.logical_not(owner))
+    def _():
+        loop(0, 64, lambda slot: settle(slot, (0, 1)))
+
     loop(0, 9, second)
+
+    @pl.when(owner)
+    def _():
+        loop(0, 64, lambda slot: settle(slot, (1,)))
+
+    outs = [
+        pltpu.make_async_copy(recv_a, out_a, out_sem.at[0]),
+        pltpu.make_async_copy(recv_b, out_b, out_sem.at[1]),
+    ]
+    for copy in outs:
+        copy.start()
 
     @pl.when(owner)
     def _():
@@ -443,21 +461,8 @@
 
     loop(0, 3, solve_row)
 
-    def late(slot):
-        settle(slot, 1)
-
-        @pl.when(jnp.logical_not(owner))
-        def _():
-            settle(slot, 0)
-
-    loop(0, 64, late)
-    outs = [
-        pltpu.make_async_copy(recv_a, out_a, out_sem.at[0]),
-        pltpu.make_async_copy(recv_b, out_b, out_sem.at[1]),
-        pltpu.make_async_copy(rows_sol, rows_out, out_sem.at[2]),
-    ]
-    for copy in outs:
-        copy.start()
+    outs.append(pltpu.make_async_copy(rows_sol, rows_out, out_sem.at[2]))
+    outs[2].start()
 
     def solve_col(n):
         h, i = n % 2, n // 2

time: 163 us -> 159 us (0.975); the launches traced: 161 us -> 159 us
  Pallas kernels: 161 us -> 159 us
    pallas_call x1, Pallas kernels: 137 us -> 134 us  [front_stage(): pl.pallas_call(front_kernel, grid=(1,), out_shape=(jax.ShapeDtypeStruct((...]
where the time goes in v4:
time: 159 us
  Pallas kernels  159 us (100%)
    pallas_call x1, Pallas kernels, front_stage(): pl.pallas_call(front_kernel, grid=(1,), out_shape=(jax.ShapeDtypeStruct((...  134 us
    pallas_call x1, Pallas kernels, final(): pl.pallas_call(final_kernel, out_shape=jax.ShapeDtypeStruct((9 * BLK, 18...  15.7 us
    pallas_call x1, Pallas kernels, pack(): pl.pallas_call(pack_kernel, out_shape=(jax.ShapeDtypeStruct((2, 4, 4, 2,...  8.77 us

profile of v4, /device:TPU:13, one launch (start us, length us, event | category | flops | bytes accessed | tf_op | source)
XLA Modules:
  0.0 158.9 jit_solution(5564515690272270775)
XLA Ops:
  0.0 8.8 %pack.1 = (bf16[2,4,4,2,2,2,128,128]{7,6,5,4,3,2,1,0:T(8,128)(2,1)}, s32[2,9]{1,0:T(2,128)}, s32[2,18]{1,0:T(2,128)}) custom-call(s32[2,64]{1,0:T(2,128)} %maps.1, bf16[2,1024,2048]{2,1,0:T(8,128)(2,1)} %children.1), custom_call_target="tpu_custom_call" | custom-call | tf_op jit(solution)/shard_map/pack/pallas_call | solution.py:61
  8.8 134.4 %front_stage.1 = (bf16[64,2,128,128]{3,2,1,0:T(8,128)(2,1)}, bf16[64,2,128,128]{3,2,1,0:T(8,128)(2,1)}, f32[9,128,256]{2,1,0:T(8,128)}, bf16[2,9,128,512]{3,2,1,0:T(8,128)(2,1)}) custom-call(s32[2,9]{1,0:T(2,128)} %get-tuple-element.12.row_tab, s32[2,18]{1,0:T(2,128)} %get-tuple-element.13.col_tab, ...), custom_call_target="tpu_custom_call" | custom-call | tf_op jit(solution)/shard_map/front_stage/pallas_call | solution.py:509
  143.2 15.7 %final.1 = f32[1152,2304]{1,0:T(8,128)} custom-call(s32[2,9]{1,0:T(2,128)} %get-tuple-element.12.row_tab, s32[2,18]{1,0:T(2,128)} %get-tuple-element.13.col_tab, bf16[8,8,2,128,128]{4,3,2,1,0:T(8,128)(2,1)} %bitcast.2, bf16[8,8,2,128,128]{4,3,2,1,0:T(8,128)(2,1)} %bitcast.8, bf16[8,8,2,128,128]{4,3,2,1,0:T(8,128)(2,1)} %bitcast.3, ...), custom_call_target="tpu_custom_call" | custom-call | tf_op jit(solution)/shard_map/final/pallas_call | solution.py:601

commit v5 on v4

--- a/solution.py
+++ b/solution.py
@@ -558,19 +558,22 @@
     own_row, own_col = lax.axis_index("row"), lax.axis_index("col")
     hi, lo = split(rows[...].reshape(3 * BLK, 2 * BLK))
     left = jnp.concatenate([hi, lo, hi], axis=1)
-    for t in range(18):
-        part = pl.ds(t * BLK, BLK)
-        right = jnp.concatenate([cols[t % 2, t // 2, :, pl.ds(k, 256)] for k in (0, 0, 256)], axis=1)
-        val = front[:, part].astype(F32) - lax.dot_general(
-            left, right, (((1,), (1,)), ((), ())), preferred_element_type=F32
+    for i in range(9):
+        right = jnp.concatenate(
+            [cols[:, i, :, pl.ds(k, 256)].reshape(2 * BLK, 2 * BLK) for k in (0, 0, 256)], axis=1
         )
-        for j in range(3):
-            here = val[j * BLK : (j + 1) * BLK]
-            for c in range(2):
-                u = col_tab[c, t]
-                blk = recv[j][c * 2 + t % 2][0, jnp.maximum(u, 0), 0].astype(F32)
-                here += jnp.where((u >= 0) & (row_tab[c, step * 3 + j] >= 0), blk, 0.0)
-            out[pl.ds(j * BLK, BLK), part] = here
+        product = lax.dot_general(left, right, (((1,), (1,)), ((), ())), preferred_element_type=F32)
+        for h in range(2):
+            t = i * 2 + h
+            part = pl.ds(t * BLK, BLK)
+            for j in range(3):
+                slot = pl.ds(j * BLK, BLK)
+                here = front[slot, part].astype(F32) - product[j * BLK : (j + 1) * BLK, h * BLK : (h + 1) * BLK]
+                for c in range(2):
+                    u = col_tab[c, t]
+                    blk = recv[j][c * 2 + h][0, jnp.maximum(u, 0), 0].astype(F32)
+                    here += jnp.where((u >= 0) & (row_tab[c, step * 3 + j] >= 0), blk, 0.0)
+                out[slot, part] = here
 
     @pl.when(own_col < 2)
     def _():

time: 159 us -> 158 us (level)
  no operation moved by 1% of the time
where the time goes in v5:
time: 158 us
  Pallas kernels  158 us (100%)
    pallas_call x1, Pallas kernels, front_stage(): pl.pallas_call(front_kernel, grid=(1,), out_shape=(jax.ShapeDtypeStruct((...  134 us
    pallas_call x1, Pallas kernels, final(): pl.pallas_call(final_kernel, out_shape=jax.ShapeDtypeStruct((9 * BLK, 18...  14.5 us
    pallas_call x1, Pallas kernels, pack(): pl.pallas_call(pack_kernel, out_shape=(jax.ShapeDtypeStruct((2, 4, 4, 2,...  8.77 us

profile of v5, /device:TPU:13, one launch (start us, length us, event | category | flops | bytes accessed | tf_op | source)
XLA Modules:
  0.0 157.7 jit_solution(9001095106662425779)
XLA Ops:
  0.0 8.8 %pack.1 = (bf16[2,4,4,2,2,2,128,128]{7,6,5,4,3,2,1,0:T(8,128)(2,1)}, s32[2,9]{1,0:T(2,128)}, s32[2,18]{1,0:T(2,128)}) custom-call(s32[2,64]{1,0:T(2,128)} %maps.1, bf16[2,1024,2048]{2,1,0:T(8,128)(2,1)} %children.1), custom_call_target="tpu_custom_call" | custom-call | tf_op jit(solution)/shard_map/pack/pallas_call | solution.py:61
  8.8 134.4 %front_stage.1 = (bf16[64,2,128,128]{3,2,1,0:T(8,128)(2,1)}, bf16[64,2,128,128]{3,2,1,0:T(8,128)(2,1)}, f32[9,128,256]{2,1,0:T(8,128)}, bf16[2,9,128,512]{3,2,1,0:T(8,128)(2,1)}) custom-call(s32[2,9]{1,0:T(2,128)} %get-tuple-element.12.row_tab, s32[2,18]{1,0:T(2,128)} %get-tuple-element.13.col_tab, ...), custom_call_target="tpu_custom_call" | custom-call | tf_op jit(solution)/shard_map/front_stage/pallas_call | solution.py:509
  143.2 14.5 %final.1 = f32[1152,2304]{1,0:T(8,128)} custom-call(s32[2,9]{1,0:T(2,128)} %get-tuple-element.12.row_tab, s32[2,18]{1,0:T(2,128)} %get-tuple-element.13.col_tab, bf16[8,8,2,128,128]{4,3,2,1,0:T(8,128)(2,1)} %bitcast.2, bf16[8,8,2,128,128]{4,3,2,1,0:T(8,128)(2,1)} %bitcast.8, bf16[8,8,2,128,128]{4,3,2,1,0:T(8,128)(2,1)} %bitcast.3, ...), custom_call_target="tpu_custom_call" | custom-call | tf_op jit(solution)/shard_map/final/pallas_call | solution.py:604
